TPU v7x, 256 devices: a whole 4x4x8 slice. The times are simulated.
256 devices in a mesh: section: 32 (over x_hi, z, core), expert: 8 (over x_lo, y).
Axes of the slice: x: 4 (x_hi: 2, x_lo: 2; x = x_hi * 2 + x_lo), y: 4, z: 8, core: 2. Of those that a mesh axis runs over, the one named last changes fastest.
Arguments:
- tokens: bfloat16 [1536, 6144], P('expert', 'section'), may hold values from -6 to 6
- expert_ids: int32 [1536, 2], P('expert'), may hold values from 0 to 7, as said below
- slot_ids: int32 [1536, 2], P('expert'), may hold values from 0 to 47, as said below
- router: float32 [6144, 8], replicated, may hold values from -0.078125 to 0.078125
- up_weight: bfloat16 [8, 6144, 8192], P('expert', None, 'section'), may hold values from -0.078125 to 0.078125
- down_weight: bfloat16 [8, 8192, 6144], P('expert', 'section'), may hold values from -0.0625 to 0.0625
- cotangent: bfloat16 [1536, 6144], P('expert', 'section'), may hold values from -6 to 6
Outputs:
- mixed: bfloat16 [1536, 6144], P('expert', 'section')
- grad_tokens: bfloat16 [1536, 6144], P('expert', 'section')
- grad_up: bfloat16 [8, 6144, 8192], P('expert', None, 'section')
- grad_down: bfloat16 [8, 8192, 6144], P('expert', 'section')
- grad_router: float32 [6144, 8], replicated
Inputs may be any that keep to these rules, and one draw needn't show every extreme that they name: `expert_ids`: within each block of 192 consecutive tokens (one group), a token's two experts differ and every expert is chosen exactly 48 times. `slot_ids`: within each block of 192 consecutive tokens, the 48 choices of one expert take the slots 0 to 47 once each.
All inputs are finite; a program needn't handle non-finite values.
Results may differ from a plain program's by a relative error of at most 0.019.
Values may be sent and summed in bfloat16 or wider, within the bound.
A program may use at most 128 MiB of HBM per device.

v0:
```python
import jax
import jax.numpy as jnp
from jax import lax
from jax.sharding import PartitionSpec as P


def gate_values(logits, choose):
    picked = jnp.sum(logits[:, None, :] * choose, axis=2)
    logit_gap = picked[:, 0] - picked[:, 1]
    return jnp.stack([jax.nn.sigmoid(logit_gap), jax.nn.sigmoid(-logit_gap)], axis=1)


def dispatch_rows(slot_place, gate_pair, rows_in, rows_cot, slot_total):
    select = (
        jnp.arange(slot_total, dtype=jnp.int32)[:, None, None] == slot_place[None, :, :]
    ).astype(jnp.float32)
    gate_row = jnp.sum(select * gate_pair[None, :, :], axis=(1, 2))
    picker = jnp.sum(select, axis=2).astype(jnp.bfloat16)
    sent_in = jnp.dot(picker, rows_in, preferred_element_type=jnp.float32).astype(jnp.bfloat16)
    sent_cot = jnp.dot(picker, rows_cot, preferred_element_type=jnp.float32)
    sent_cot = (sent_cot * gate_row[:, None]).astype(jnp.bfloat16)
    return (sent_in, sent_cot)


def shards(tokens, expert_ids, slot_ids, router, up_weight, down_weight, cotangent):
    token_count, feat_slice = tokens.shape
    model_width, n_expert = router.shape
    slot_cap = 2 * token_count // n_expert
    slot_total = n_expert * slot_cap
    feat_start = lax.axis_index("section") * feat_slice
    router_rows = lax.dynamic_slice_in_dim(router, feat_start, feat_slice, 0)
    choose = (
        expert_ids[:, :, None] == jnp.arange(n_expert, dtype=jnp.int32)[None, None, :]
    ).astype(jnp.float32)
    slot_place = expert_ids * slot_cap + slot_ids
    full_in, full_cot = (
        lax.all_gather(tokens, "section", axis=1, tiled=True),
        lax.all_gather(cotangent, "section", axis=1, tiled=True),
    )
    logits = jnp.dot(full_in.astype(jnp.float32), router, precision=lax.Precision.HIGHEST)
    gate_pair = gate_values(logits, choose)
    sent_in, sent_cot = dispatch_rows(slot_place, gate_pair, full_in, full_cot, slot_total)
    block_shape = (n_expert, slot_cap, model_width)
    rows_in, rows_cot = (
        lax.all_to_all(
            sent_in.reshape(block_shape), "expert", split_axis=0, concat_axis=0, tiled=True
        ),
        lax.all_to_all(
            sent_cot.reshape(block_shape), "expert", split_axis=0, concat_axis=0, tiled=True
        ),
    )
    rows_in = rows_in.reshape(slot_total, model_width)
    rows_cot = rows_cot.reshape(slot_total, model_width)
    weight_in = up_weight[0]
    weight_out = down_weight[0]
    pre_act = jnp.dot(rows_in, weight_in, preferred_element_type=jnp.float32)
    sigma = jax.nn.sigmoid(pre_act)
    hidden = (pre_act * sigma).astype(jnp.bfloat16)
    hidden_grad = lax.dot_general(
        rows_cot, weight_out, (((1,), (1,)), ((), ())), preferred_element_type=jnp.float32
    )
    pre_grad = (hidden_grad * sigma * (1.0 + pre_act * (1.0 - sigma))).astype(jnp.bfloat16)
    grad_down = lax.dot_general(
        hidden, rows_cot, (((0,), (0,)), ((), ())), preferred_element_type=jnp.float32
    ).astype(jnp.bfloat16)
    grad_up = lax.dot_general(
        rows_in, pre_grad, (((0,), (0,)), ((), ())), preferred_element_type=jnp.float32
    ).astype(jnp.bfloat16)
    forward_part = jnp.dot(hidden, weight_out, preferred_element_type=jnp.float32)
    backward_part = lax.dot_general(
        pre_grad, weight_in, (((1,), (1,)), ((), ())), preferred_element_type=jnp.float32
    )
    out_sum, back_sum = (
        lax.psum_scatter(
            forward_part.astype(jnp.bfloat16), "section", scatter_dimension=1, tiled=True
        ).astype(jnp.float32),
        lax.psum_scatter(
            backward_part.astype(jnp.bfloat16), "section", scatter_dimension=1, tiled=True
        ).astype(jnp.float32),
    )
    return_shape = (n_expert, slot_cap, feat_slice)
    came_out, came_back = (
        lax.all_to_all(
            out_sum.astype(jnp.bfloat16).reshape(return_shape),
            "expert",
            split_axis=0,
            concat_axis=0,
            tiled=True,
        ),
        lax.all_to_all(
            back_sum.astype(jnp.bfloat16).reshape(return_shape),
            "expert",
            split_axis=0,
            concat_axis=0,
            tiled=True,
        ),
    )
    flat_out = came_out.reshape(slot_total, feat_slice)
    flat_back = came_back.reshape(slot_total, feat_slice)
    positions = jnp.arange(slot_total, dtype=jnp.int32)
    take_first = (slot_place[:, 0:1] == positions[None, :]).astype(jnp.bfloat16)
    take_second = (slot_place[:, 1:2] == positions[None, :]).astype(jnp.bfloat16)
    out_first = jnp.dot(take_first, flat_out, preferred_element_type=jnp.float32)
    out_second = jnp.dot(take_second, flat_out, preferred_element_type=jnp.float32)
    mixed = gate_pair[:, 0:1] * out_first + gate_pair[:, 1:2] * out_second
    cot_float = cotangent.astype(jnp.float32)
    grad_first, grad_second = lax.psum(
        (jnp.sum(cot_float * out_first, axis=1), jnp.sum(cot_float * out_second, axis=1)), "section"
    )
    logit_grad = (grad_first - grad_second) * gate_pair[:, 0] * gate_pair[:, 1]
    logits_grad = (choose[:, 0, :] - choose[:, 1, :]) * logit_grad[:, None]
    back_first = jnp.dot(take_first, flat_back, preferred_element_type=jnp.float32)
    back_second = jnp.dot(take_second, flat_back, preferred_element_type=jnp.float32)
    grad_tokens = (
        back_first
        + back_second
        + jnp.dot(logits_grad, router_rows.T, precision=lax.Precision.HIGHEST)
    )
    local_router = jnp.dot(
        tokens.astype(jnp.float32).T, logits_grad, precision=lax.Precision.HIGHEST
    )
    placed_router = lax.dynamic_update_slice(
        jnp.zeros((model_width, n_expert), jnp.float32), local_router, (feat_start, jnp.int32(0))
    )
    grad_router = lax.psum(placed_router, ("section", "expert"))
    return (
        mixed.astype(jnp.bfloat16),
        grad_tokens.astype(jnp.bfloat16),
        grad_up[None],
        grad_down[None],
        grad_router,
    )


def solution(mesh):
    in_specs = (
        P("expert", "section"),
        P("expert", None),
        P("expert", None),
        P(),
        P("expert", None, "section"),
        P("expert", "section", None),
        P("expert", "section"),
    )
    out_specs = (
        P("expert", "section"),
        P("expert", "section"),
        P("expert", None, "section"),
        P("expert", "section", None),
        P(),
    )
    return jax.shard_map(shards, mesh=mesh, in_specs=in_specs, out_specs=out_specs, check_vma=False)
```

profile of v0, /device:TPU:1, one launch (start us, length us, event | category | flops | bytes accessed | tf_op | source)
XLA Modules:
  0.0 798.1 jit_solution(7832499318834523150)
XLA Ops:
  7.2 0.0 all-gather.3.cloned.1.call-start
  7.2 1.8 copy.35
  9.0 0.7 multiply_add_fusion
  9.7 88.7 %all-gather.3.cloned.1.call-done = bf16[192,6144]{0,1:T(8,128)(2,1)} async-done(((bf16[192,192]{0,1:T(8,128)(2,1)}), bf16[192,6144]{0,1:T(8,128)(2,1)}) %all-gather.3.cloned.1.call-update) | async-done | bytes 2359312 | tf_op jit(solution)/shard_map/all_gather | solution.py:37
  98.5 3.4 fusion.39
  101.8 0.7 select_reduce_fusion.1
  102.6 0.5 copy-done.10
  103.2 0.2 select_reduce_fusion
  103.4 3.7 convolution_convert_fusion.2
  107.0 4.7 all-to-all-start
  111.8 0.0 all-gather.5.cloned.1.call-start
  111.8 0.7 copy.37
  112.6 0.0 reduce-scatter.3.cloned.1.call-start
  112.6 53.5 %all-to-all-done = bf16[8,48,6144]{2,1,0:T(8,128)(2,1)} async-done(((bf16[8,48,6144]{2,1,0:T(8,128)(2,1)}), bf16[8,48,6144]{2,1,0:T(8,128)(2,1)}, u32[]{:S(2)}, u32[]{:S(2)}) %all-to-all-start) | async-done | bytes 4718624 | tf_op jit(solution)/shard_map/all_to_all | solution.py:45
  166.2 4.7 fusion.6
  170.9 4.1 convolution_convert_fusion.1
  175.0 0.0 reduce-scatter.5.cloned.1.call-start
  175.1 21.7 %all-gather.5.cloned.1.call-done = bf16[192,6144]{0,1:T(8,128)(2,1)} async-done(((bf16[192,192]{0,1:T(8,128)(2,1)}), bf16[192,6144]{0,1:T(8,128)(2,1)}) %all-gather.5.cloned.1.call-update) | async-done | bytes 2359312 | tf_op jit(solution)/shard_map/all_gather | solution.py:38
  196.7 3.8 multiply_convert_fusion
  200.6 61.3 %all_to_all.20 = bf16[8,48,6144]{2,1,0:T(8,128)(2,1)S(1)} all-to-all(bf16[8,48,6144]{2,1,0:T(8,128)(2,1)S(1)} %bitcast.60), channel_id=1, replica_groups=mesh['section'=32,'expert'=8] {'expert'}, dimensions={0} | all-to-all | bytes 9437184 | tf_op jit(solution)/shard_map/all_to_all | solution.py:48
  261.9 2.1 copy-done.1
  264.0 1.4 fusion.14
  265.4 0.7 copy-done.6
  266.1 4.0 convolution_convert_fusion
  270.2 0.6 fusion.38
  270.8 0.7 fusion.30
  271.4 5.9 fusion
  277.3 49.2 %reduce-scatter.3.cloned.1.call-done = bf16[384,192]{0,1:T(8,128)(2,1)} async-done(((bf16[384,6144]{0,1:T(8,128)(2,1)}), bf16[384,192]{0,1:T(8,128)(2,1)}) %reduce-scatter.3.cloned.1.call-update) | async-done | bytes 147472 | tf_op jit(solution)/shard_map/reduce_scatter | solution.py:74
  326.5 1.7 copy.36
  328.2 4.9 all-to-all-start.1
  333.1 5.9 fusion.1
  338.9 121.7 %reduce-scatter.5.cloned.1.call-done = bf16[384,192]{0,1:T(8,128)(2,1)} async-done(((bf16[384,6144]{0,1:T(8,128)(2,1)}), bf16[384,192]{0,1:T(8,128)(2,1)}) %reduce-scatter.5.cloned.1.call-update) | async-done | bytes 147472 | tf_op jit(solution)/shard_map/reduce_scatter | solution.py:77
  460.6 1.7 copy.38
  462.3 3.8 all-to-all-start.3
  466.2 1.2 fusion.21
  467.4 2.0 fusion.23
  469.4 70.1 %all-reduce = (f32[192]{0:T(256)S(1)}, f32[192]{0:T(256)S(1)}) all-reduce(f32[192]{0:T(256)S(1)} %get-tuple-element.26, f32[192]{0:T(256)S(1)} %get-tuple-element.25), channel_id=1, replica_groups=mesh['section'=32,'expert'=8] {'section'}, use_global_device_ids=true, to_apply=%region_6.0 | all-reduce | flops 384 | bytes 3072 | tf_op jit(solution)/shard_map/psum | solution.py:107
  539.4 0.7 multiply_multiply_fusion
  540.1 0.6 copy-done.8
  540.7 1.7 convolution_bitcast_fusion
  542.3 0.9 dynamic_update_slice.3
  543.3 0.7 copy-done.5
  544.0 1.1 fusion.33
  545.1 0.9 fusion.20
  546.0 1.6 fusion.18
  547.6 1.6 copy.40
  549.2 240.7 %all-reduce.3.cloned.1.call-done = f32[6144,8]{0,1:T(8,128)} async-done(((f32[6144,8]{0,1:T(8,128)}), f32[6144,8]{0,1:T(8,128)}) %all-reduce.3.cloned.1.call-update) | async-done | bytes 196624 | tf_op jit(solution)/shard_map/psum | solution.py:125
  789.9 1.6 copy.43
  (29 shorter events, 0.2 us)
Async XLA Ops:
  7.2 163.7 %copy-start = (bf16[1,256,6144]{2,1,0:T(8,128)(2,1)S(1)}, bf16[1,256,6144]{2,1,0:T(8,128)(2,1)}, u32[]{:S(2)}) copy-start(bf16[1,256,6144]{2,1,0:T(8,128)(2,1)} %param.12) | copy-start | bytes 9437188
  7.2 91.3 %all-gather.3.cloned.1.call-start = ((), (), s32[]{:S(2)}) async-start(), calls=%async_computation.6 | async-start | bytes 3244032 | tf_op jit(solution)/shard_map/all_gather | solution.py:37
  98.5 4.9 copy-start.2
  102.6 0.6 copy-start.10
  102.6 0.6 copy-start.9
  103.3 3.7 copy-start.4
  107.0 4.8 copy-start.7
  107.0 59.1 %all-to-all-start = ((bf16[8,48,6144]{2,1,0:T(8,128)(2,1)}), bf16[8,48,6144]{2,1,0:T(8,128)(2,1)}, u32[]{:S(2)}, u32[]{:S(2)}) async-start(bf16[8,48,6144]{2,1,0:T(8,128)(2,1)} %bitcast.59), calls=%async_computation | async-start | bytes 9437184 | tf_op jit(solution)/shard_map/all_to_all | solution.py:45
  111.8 85.0 %all-gather.5.cloned.1.call-start = ((), (), s32[]{:S(2)}) async-start(), calls=%async_computation.8 | async-start | bytes 3244032 | tf_op jit(solution)/shard_map/all_gather | solution.py:38
  112.6 213.9 %reduce-scatter.3.cloned.1.call-start = ((), (), s32[]{:S(2)}) async-start(), calls=%async_computation.7 | async-start | bytes 4866048 | tf_op jit(solution)/shard_map/reduce_scatter | solution.py:74
  175.0 285.6 %reduce-scatter.5.cloned.1.call-start = ((), (), s32[]{:S(2)}) async-start(), calls=%async_computation.9 | async-start | bytes 4866048 | tf_op jit(solution)/shard_map/reduce_scatter | solution.py:77
  261.9 2.1 copy-start.1
  264.0 2.1 copy-start.3
  265.4 0.7 copy-start.6
  328.2 134.1 %all-to-all-start.1 = ((bf16[8,48,192]{2,1,0:T(8,128)(2,1)}), bf16[8,48,192]{2,1,0:T(8,128)(2,1)}, u32[]{:S(2)}, u32[]{:S(2)}) async-start(bf16[8,48,192]{2,1,0:T(8,128)(2,1)} %bitcast.63), calls=%async_computation.2 | async-start | bytes 393216 | tf_op jit(solution)/shard_map/all_to_all | solution.py:83
  462.3 82.7 %all-to-all-start.3 = ((bf16[8,48,192]{2,1,0:T(8,128)(2,1)}), bf16[8,48,192]{2,1,0:T(8,128)(2,1)S(1)}, u32[]{:S(2)}, u32[]{:S(2)}) async-start(bf16[8,48,192]{2,1,0:T(8,128)(2,1)} %bitcast.12), calls=%async_computation.5 | async-start | bytes 393216 | tf_op jit(solution)/shard_map/all_to_all | solution.py:90
  466.1 323.8 %all-reduce.3.cloned.1.call-start = ((), (), s32[]{:S(2)}) async-start(), calls=%async_computation.10 | async-start | bytes 393216 | tf_op jit(solution)/shard_map/psum | solution.py:125
  540.1 0.6 copy-start.8
  543.3 0.7 copy-start.5
Sparse Core Ops, SparseCore 0:
  11.3 87.0 all-gather.2
  115.9 80.7 all-gather.4
  201.0 125.4 reduce-scatter.2
  330.6 129.9 reduce-scatter.4
  544.1 245.8 all-reduce.2
where the time goes:
time: 799 us; the launch traced here: 798 us
  waiting for transfers between devices  576 us (72%)
  blocking collectives  131 us (16%)
  matrix products  45.3 us (6%)
  local copies, waits for them, and re-layouts  15.4 us (2%)
  between operations  14 us (2%)
  starting transfers between devices  13.5 us (2%)
    psum x1, waiting for transfers between devices, shards(): grad_router = lax.psum(placed_router, ('section', 'expert'))  241 us
    reduce_scatter x1, waiting for transfers between devices, shards(): lax.psum_scatter(backward_part.astype(jnp.bfloat16), 'section', scatter_d...  122 us
    all_gather x1, waiting for transfers between devices, shards(): lax.all_gather(tokens, 'section', axis=1, tiled=True)  88.7 us
    psum x1, blocking collectives, shards(): lax.psum((jnp.sum(cot_float * out_first, axis=1), jnp.sum(cot_float * out...  70.1 us
    all_to_all x1, blocking collectives, shards(): lax.all_to_all(sent_cot.reshape(block_shape), 'expert', split_axis=0, con...  61.3 us
    all_to_all x1, waiting for transfers between devices, shards(): lax.all_to_all(sent_in.reshape(block_shape), 'expert', split_axis=0, conc...  53.5 us
    reduce_scatter x1, waiting for transfers between devices, shards(): lax.psum_scatter(forward_part.astype(jnp.bfloat16), 'section', scatter_di...  49.2 us
    all_gather x1, waiting for transfers between devices, shards(): lax.all_gather(cotangent, 'section', axis=1, tiled=True)  21.7 us
  transfers between devices with their start and end apart: 8, of which 6 were waited for; matrix products, arithmetic and copies ran while one was open for 6% of the time, Pallas kernels for 0%

commit v1 on v0

v1 whole, which is shorter than its diff:
```python
import jax
import jax.numpy as jnp
from jax import lax
from jax.experimental import pallas as pl
from jax.experimental.pallas import tpu as pltpu
from jax.sharding import PartitionSpec as P

MESH = pl.DeviceIdType.MESH
NZ = 8
FAR = NZ // 2
NE = 8
CAP = 48
TOK = 192
FEAT = 192
BLK = 2 * FEAT
ROWS = NE * CAP
HALF = ROWS // 2
QUART = HALF // 2
HID = 256
WIDTH = 6144
NBLK = WIDTH // BLK
BF = jnp.bfloat16
F32 = jnp.float32
LO = pl.ds(0, HALF)
HI = pl.ds(HALF, HALF)


def dot_nn(a, b):
    return jnp.dot(a, b, preferred_element_type=F32)


def dot_nt(a, b):
    return lax.dot_general(a, b, (((1,), (1,)), ((), ())), preferred_element_type=F32)


def dot_tn(a, b):
    return lax.dot_general(a, b, (((0,), (0,)), ((), ())), preferred_element_type=F32)


def lanes(p):
    return pl.ds(pl.multiple_of(p * BLK, BLK), BLK)


def rows_of(q):
    return pl.ds(pl.multiple_of(q * CAP, CAP), CAP)


def kernel(
    keep_ref, give_ref, ids_ref, slots_ref, rt_ref, up_ref, dn_ref,
    om_ref, og_ref, gu_ref, gd_ref, gr_ref,
    gath, wu, wd, gu, gd, rt3, pick, xch, sent, msend, meta,
    pre, logit, ms, mr, pg, tsb, tlb, part,
    ta_s, ta_r, tb_s, tb_r, tp_s, tp_r, xs, xr,
    fs0, fs1, ret0, ret1, outs, outr,
    gp, g1, g2s, g2, g3s, g3,
    w_sem, x_sem, d_ssem, d_rsem, m_ssem, m_rsem,
    a_ssem, a_rsem, b_ssem, b_rsem, p_ssem, p_rsem, f_ssem, f_rsem,
    mid_sem, ra_ssem, ra_rsem, rb_ssem, rb_rsem, rp_ssem, rp_rsem, rx_ssem, rx_rsem,
    gsem, r_ssem, r_rsem, q_ssem, q_rsem, o_sem,
    g1_ssem, g1_rsem, g2_ssem, g2_rsem, g3_ssem, g3_rsem, g4_sem,
):
    s = lax.axis_index("section")
    q = lax.axis_index("expert")
    c = lax.rem(s, 2)
    z = lax.rem(s // 2, NZ)
    h = s // (2 * NZ)

    def dev(hh, zz, cc, qq):
        return ((hh * NZ + zz) * 2 + cc, qq)

    def zwrap(v):
        return lax.rem(v + 2 * NZ, NZ)

    def qwrap(v):
        return lax.rem(v + NE, NE)

    sib = dev(h, z, 1 - c, q)
    partner = dev(1 - h, z, c, q)
    zdev = (dev(h, zwrap(z + 1), c, q), dev(h, zwrap(z - 1), c, q))

    def znext(d):
        return dev(h, zwrap(z + 1 - 2 * d), c, q)

    def rcopy(src, dst, ssem, rsem, target):
        return pltpu.make_async_remote_copy(
            src_ref=src, dst_ref=dst, send_sem=ssem, recv_sem=rsem, device_id=target, device_id_type=MESH
        )

    barrier = pltpu.get_barrier_semaphore()
    peers = [sib]
    for dh in range(2):
        for dq in range(NE):
            if dh or dq:
                peers.append(dev(lax.rem(h + dh, 2), z, c, qwrap(q + dq)))
    for dz in range(1, NZ):
        peers.append(dev(h, zwrap(z + dz), c, q))
    for peer in peers:
        pl.semaphore_signal(barrier, inc=1, device_id=peer, device_id_type=MESH)
    pl.semaphore_wait(barrier, len(peers))

    trade = rcopy(give_ref, xch, x_sem.at[0], x_sem.at[1], sib)
    trade.start()

    w_in = pltpu.make_async_copy(up_ref, wu.at[0], w_sem.at[0])
    w_in_give = rcopy(dn_ref, wd.at[0], w_sem.at[1], w_sem.at[2], sib)
    w_out = pltpu.make_async_copy(dn_ref, wd.at[1], w_sem.at[0])
    w_out_give = rcopy(up_ref, wu.at[1], w_sem.at[1], w_sem.at[2], sib)

    @pl.when(c == 0)
    def _():
        w_in.start()
        w_in_give.start()

    @pl.when(c == 1)
    def _():
        w_out.start()
        w_out_give.start()

    place0 = ids_ref[0:1, :] * CAP + slots_ref[0:1, :]
    place1 = ids_ref[1:2, :] * CAP + slots_ref[1:2, :]
    slot = lax.broadcasted_iota(jnp.int32, (ROWS, TOK), 0)
    hit0 = (slot == place0).astype(F32)
    hit1 = (slot == place1).astype(F32)
    pick[...] = (hit0 + hit1).astype(BF)
    lane8 = lax.broadcasted_iota(jnp.int32, (128, TOK), 0)
    expert = lax.rem(lane8, NE)
    live = lane8 < 3 * NE
    sign = jnp.where(live & (expert == ids_ref[0:1, :]), 1.0, 0.0) - jnp.where(
        live & (expert == ids_ref[1:2, :]), 1.0, 0.0
    )

    @pl.when(c == 0)
    def _():
        msend[...] = dot_nt((hit0 - hit1).astype(BF), sign.astype(BF)).astype(BF)

    ta_r[1, 1] = jnp.zeros((HALF, BLK), BF)
    tb_r[0, 1] = jnp.zeros((HALF, BLK), BF)
    tp_r[0, 1, pl.ds(QUART, QUART)] = jnp.zeros((QUART, BLK), BF)
    tp_r[1, 1, pl.ds(0, QUART)] = jnp.zeros((QUART, BLK), BF)
    pre[...] = jnp.zeros((ROWS, 2 * HID), F32)
    logit[...] = jnp.zeros((ROWS, 128), F32)

    trade.wait_recv()
    both = keep_ref[...] + xch[...]
    sent[...] = dot_nn(pick[...], both).astype(BF)

    mine = h * NZ + z

    def disp(dh, dq):
        qd = qwrap(q + dq)
        return rcopy(
            sent.at[rows_of(qd)], gath.at[mine, rows_of(q)], d_ssem.at[dh, dq], d_rsem.at[dh, dq],
            dev(lax.rem(h + dh, 2), z, c, qd),
        )

    def disp_land(dh, dq):
        land = gath.at[lax.rem(h + dh, 2) * NZ + z, rows_of(qwrap(q - dq))]
        return rcopy(land, land, d_ssem.at[dh, dq], d_rsem.at[dh, dq], sib)

    def meta_copy(dq):
        qd = qwrap(q + dq)
        return rcopy(
            msend.at[rows_of(qd)], meta.at[rows_of(q)], m_ssem.at[dq], m_rsem.at[dq], dev(h, z, c, qd)
        )

    def meta_land(dq):
        land = meta.at[rows_of(qwrap(q - dq))]
        return rcopy(land, land, m_ssem.at[dq], m_rsem.at[dq], sib)

    @pl.when(q < NE // 2)
    def _():
        for dq in range(NE):
            disp(1, dq).start()

    for dq in range(1, NE):
        disp(0, dq).start()

    @pl.when(c == 0)
    def _():
        for dq in range(1, NE):
            meta_copy(dq).start()
        meta[rows_of(q), :] = msend[rows_of(q), :]

    gath[mine, rows_of(q), :] = sent[rows_of(q), :]

    def zblock(hh, d, k):
        return hh * NZ + zwrap(z - k + 2 * d * k)

    def copy_a(d, k):
        ref = gath.at[zblock(h, d, k - 1), LO]
        return rcopy(ref, ref, a_ssem.at[d, k], a_rsem.at[d, k], znext(d))

    def land_a(d, k):
        ref = gath.at[zblock(h, d, k), LO]
        return rcopy(ref, ref, a_ssem.at[d, k], a_rsem.at[d, k], znext(d))

    def copy_b(d, k):
        ref = gath.at[zblock(h, d, k - 1), HI]
        return rcopy(ref, ref, b_ssem.at[d, k], b_rsem.at[d, k], znext(d))

    def land_b(d, k):
        ref = gath.at[zblock(h, d, k), HI]
        return rcopy(ref, ref, b_ssem.at[d, k], b_rsem.at[d, k], znext(d))

    def part_p(d, far):
        return pl.ds(d * QUART, QUART) if far else LO

    def copy_p(d, k, far):
        ref = gath.at[zblock(1 - h, d, k - 1), part_p(d, far)]
        return rcopy(ref, ref, p_ssem.at[d, k], p_rsem.at[d, k], znext(d))

    def land_p(d, k, far):
        ref = gath.at[zblock(1 - h, d, k), part_p(d, far)]
        return rcopy(ref, ref, p_ssem.at[d, k], p_rsem.at[d, k], znext(d))

    def copy_f(d, k):
        ref = gath.at[zblock(h, d, k), HI]
        return rcopy(ref, ref, f_ssem.at[d, k], f_rsem.at[d, k], partner)

    def land_f(d, k):
        ref = gath.at[zblock(1 - h, d, k), HI]
        return rcopy(ref, ref, f_ssem.at[d, k], f_rsem.at[d, k], partner)

    for dq in range(1, NE):
        disp_land(0, dq).wait_recv()
    for d in range(2):
        copy_a(d, 1).start()
        copy_b(d, 1).start()
    copy_f(0, 0).start()
    for dq in range(NE):

        @pl.when(qwrap(q - dq) < NE // 2)
        def _():
            disp_land(1, dq).wait_recv()

    for d in range(2):
        copy_p(d, 1, False).start()

    @pl.when(c == 0)
    def _():
        def split(p, carry):
            r = rt_ref[:, lanes(p)]
            top = r.astype(BF).astype(F32)
            mid = (r - top).astype(BF).astype(F32)
            low = r - top - mid
            rt3[:, lanes(p)] = jnp.concatenate([top, mid, low, jnp.zeros((104, BLK), F32)], axis=0).astype(BF)
            return carry

        lax.fori_loop(0, NBLK, split, 0)
        w_in.wait()
        w_out_give.wait_recv()
        for dq in range(1, NE):
            meta_land(dq).wait_recv()

    @pl.when(c == 1)
    def _():
        w_out.wait()
        w_in_give.wait_recv()

    def accumulate(p):
        @pl.when(c == 0)
        def _():
            x = gath[p]
            pre[:, 0:HID] += dot_nn(x, wu[0, lanes(p), :])
            pre[:, HID : 2 * HID] += dot_nn(x, wu[1, lanes(p), :])
            logit[...] += dot_nt(x, rt3[:, lanes(p)])

        @pl.when(c == 1)
        def _():
            x = gath[p]
            pre[:, 0:HID] += dot_nt(x, wd[0, :, lanes(p)])
            pre[:, HID : 2 * HID] += dot_nt(x, wd[1, :, lanes(p)])

    def gather_step(k, carry):
        near = k < FAR

        @pl.when((k >= 1) & (k <= FAR))
        def _():
            land_a(0, k).wait_recv()

            @pl.when(near)
            def _():
                copy_a(0, k + 1).start()

            land_b(1, k).wait_recv()

            @pl.when(near)
            def _():
                copy_b(1, k + 1).start()

            copy_f(1, k).start()

            @pl.when(near)
            def _():
                land_a(1, k).wait_recv()

                @pl.when(k < FAR - 1)
                def _():
                    copy_a(1, k + 1).start()

                land_b(0, k).wait_recv()

                @pl.when(k < FAR - 1)
                def _():
                    copy_b(0, k + 1).start()

                copy_f(0, k).start()
                for d in range(2):
                    land_p(d, k, False).wait_recv()

                    @pl.when(k < FAR - 1)
                    def _():
                        copy_p(d, k + 1, False).start()

                    @pl.when(k == FAR - 1)
                    def _():
                        copy_p(d, k + 1, True).start()

            @pl.when(k == FAR)
            def _():
                for d in range(2):
                    land_p(d, k, True).wait_recv()

        def block_step(j, carry2):
            d = lax.rem(j, 2)
            other = j // 2
            dist = k - other
            ok = (dist >= 0) & (dist <= FAR)
            ok = ok & ((d == 0) | ((dist >= 1) & (dist < FAR)))

            @pl.when(ok)
            def _():
                @pl.when(other == 1)
                def _():
                    dx = jnp.where(dist == FAR, 1, d)
                    land_f(dx, dist).wait_recv()

                accumulate(zblock(lax.rem(h + other, 2), d, dist))

            return carry2

        lax.fori_loop(0, 4, block_step, 0)
        return carry

    lax.fori_loop(0, FAR + 2, gather_step, 0)

    middle = rcopy(ms, mr, mid_sem.at[0], mid_sem.at[1], sib)

    @pl.when(c == 1)
    def _():
        ms[...] = pre[...].astype(BF)

    def gates():
        gap = jnp.sum(logit[...] * meta[...].astype(F32), axis=1, keepdims=True)
        return jax.nn.sigmoid(gap), jax.nn.sigmoid(-gap)

    @pl.when(c == 0)
    def _():
        gate, _ = gates()
        v = pre[...]
        ms[...] = (gate * (v * jax.nn.sigmoid(v))).astype(BF)

    middle.start()
    middle.wait_recv()

    @pl.when(c == 0)
    def _():
        gate, gate_other = gates()
        v = pre[...]
        u = mr[...].astype(F32)
        sg = jax.nn.sigmoid(v)
        pg[...] = (gate * u * (sg * (1.0 + v * (1.0 - sg)))).astype(BF)
        t = jnp.sum(v * sg * u, axis=1, keepdims=True) * gate * gate_other
        ts = t * meta[...].astype(F32)
        top = ts.astype(BF).astype(F32)
        lane = lax.broadcasted_iota(jnp.int32, (ROWS, 128), 1)
        tsb[...] = ts.astype(BF)
        tlb[...] = jnp.where(lane < NE, top, jnp.where(lane < 2 * NE, ts - top, 0.0)).astype(BF)

    def product(p, r):
        @pl.when(c == 0)
        def _():
            acc = dot_nt(pg[r, 0:HID], wu[0, lanes(p), :])
            acc += dot_nt(pg[r, HID : 2 * HID], wu[1, lanes(p), :])
            part[...] = acc + dot_nn(tsb[r, :], rt3[:, lanes(p)])

        @pl.when(c == 1)
        def _():
            acc = dot_nn(mr[r, 0:HID], wd[0, :, lanes(p)])
            part[...] = acc + dot_nn(mr[r, HID : 2 * HID], wd[1, :, lanes(p)])

    def tblock(hh, d, dist):
        return hh * NZ + zwrap(z + dist - 2 * d * dist)

    def copy_ra(d, t):
        return rcopy(ta_s.at[d, t], ta_r.at[d, t], ra_ssem.at[d, t], ra_rsem.at[d, t], znext(d))

    def copy_rb(d, t):
        return rcopy(tb_s.at[d, t], tb_r.at[d, t], rb_ssem.at[d, t], rb_rsem.at[d, t], znext(d))

    def copy_rp(d, t, far):
        rr = part_p(d, far)
        return rcopy(tp_s.at[d, t, rr], tp_r.at[d, t, rr], rp_ssem.at[d, t], rp_rsem.at[d, t], znext(d))

    def copy_rx(d, dist):
        return rcopy(xs.at[d, dist], xr.at[d, dist], rx_ssem.at[d, dist], rx_rsem.at[d, dist], partner)

    def wait_rp(d, t):
        @pl.when(t == 1)
        def _():
            copy_rp(d, 1, True).wait_recv()

        @pl.when(t > 1)
        def _():
            copy_rp(d, t, False).wait_recv()

    plane = [(dh, dq) for dh in range(2) for dq in range(NE) if dh or dq]

    def plane_dev(dh, dq):
        return lax.rem(h + dh, 2), qwrap(q + dq)

    def copy_g1(i, dh, dq):
        hh, qq = plane_dev(dh, dq)
        return rcopy(gp.at[hh * NE + qq], g1.at[i], g1_ssem.at[i], g1_rsem.at[i], dev(hh, z, c, qq))

    def copy_g2(dz):
        return rcopy(g2s, g2.at[dz], g2_ssem.at[dz], g2_rsem.at[dz], dev(h, zwrap(z + dz), c, q))

    me_p = h * NE + q

    def copy_g3(i, dh, dq):
        hh, qq = plane_dev(dh, dq)
        return rcopy(g3s, g3.at[me_p], g3_ssem.at[i], g3_rsem.at[i], dev(hh, z, c, qq))

    def land_g3(i, dh, dq):
        hh, qq = lax.rem(h + dh, 2), qwrap(q - dq)
        return rcopy(g3s, g3.at[hh * NE + qq], g3_ssem.at[i], g3_rsem.at[i], sib)

    g4 = rcopy(g3, gr_ref, g4_sem.at[0], g4_sem.at[1], sib)

    def router_stage(step):
        @pl.when((c == 0) & (step == 0))
        def _():
            tl = tlb[...]

            def one(p, carry):
                full = dot_tn(tl, gath[p])
                gp[p] = full[0:NE] + full[NE : 2 * NE]
                return carry

            lax.fori_loop(0, NBLK, one, 0)
            for i, (dh, dq) in enumerate(plane):
                copy_g1(i, dh, dq).start()

        @pl.when((c == 0) & (step == 2))
        def _():
            total = gp[me_p]
            for i, (dh, dq) in enumerate(plane):
                copy_g1(i, dh, dq).wait_recv()
                total = total + g1[i]
            g2s[...] = total
            for dz in range(1, NZ):
                copy_g2(dz).start()

        @pl.when((c == 0) & (step == 3))
        def _():
            total = g2s[...]
            for dz in range(1, NZ):
                copy_g2(dz).wait_recv()
                total = total + g2[dz]
            g3s[...] = total
            g3[me_p] = total
            for i, (dh, dq) in enumerate(plane):
                copy_g3(i, dh, dq).start()

        @pl.when((c == 0) & (step == 4))
        def _():
            for i, (dh, dq) in enumerate(plane):
                land_g3(i, dh, dq).wait_recv()
            g4.start()

    gu_own = pltpu.make_async_copy(gu.at[0], gu_ref, gsem.at[0])
    gu_give = rcopy(gu.at[1], gu_ref, gsem.at[1], gsem.at[2], sib)
    gd_own = pltpu.make_async_copy(gd.at[1], gd_ref, gsem.at[0])
    gd_give = rcopy(gd.at[0], gd_ref, gsem.at[1], gsem.at[2], sib)

    def weight_grads(step):
        def one(i, carry):
            p = step * 4 + i

            @pl.when(c == 0)
            def _():
                full = dot_tn(gath[p], pg[...]).astype(BF)
                gu[0, lanes(p), :] = full[:, 0:HID]
                gu[1, lanes(p), :] = full[:, HID : 2 * HID]

            @pl.when(c == 1)
            def _():
                full = dot_tn(mr[...], gath[p]).astype(BF)
                gd[0, :, lanes(p)] = full[0:HID]
                gd[1, :, lanes(p)] = full[HID : 2 * HID]

            return carry

        @pl.when(step < 4)
        def _():
            lax.fori_loop(0, 4, one, 0)

        @pl.when((step == 3) & (c == 0))
        def _():
            gu_own.start()
            gu_give.start()

        @pl.when((step == 3) & (c == 1))
        def _():
            gd_own.start()
            gd_give.start()

    last = FAR + 1

    def scatter_step(step, carry):
        dist = last - step
        nxt = FAR - step

        def side(d, carry2):
            @pl.when(((step == 0) & (d == 1)) | ((step >= 1) & (step < FAR)) | ((step == FAR) & (d == 0)))
            def _():
                product(tblock(1 - h, d, nxt), HI)
                xs[d, nxt] = part[...].astype(BF)
                copy_rx(d, nxt).start()

            @pl.when((((step == 1) | (step == last)) & (d == 0)) | ((step > 1) & (step < last)))
            def _():
                product(tblock(h, d, dist), LO)

                @pl.when(step == 1)
                def _():
                    ta_s[0, 1] = part[...].astype(BF)
                    copy_ra(0, 1).start()

                @pl.when((step > 1) & (step < last))
                def _():
                    @pl.when((step > 2) | (d == 0))
                    def _():
                        copy_ra(d, step - 1).wait_recv()

                    ta_s[d, step] = (part[...] + ta_r[d, step - 1].astype(F32)).astype(BF)
                    copy_ra(d, step).start()

                @pl.when(step == last)
                def _():
                    copy_ra(0, FAR).wait_recv()
                    copy_ra(1, FAR).wait_recv()
                    fs0[LO, :] = (part[...] + ta_r[0, FAR].astype(F32) + ta_r[1, FAR].astype(F32)).astype(BF)

            @pl.when((((step == 1) | (step == last)) & (d == 0)) | ((step > 1) & (step < last)))
            def _():
                product(tblock(1 - h, d, dist), LO)

                @pl.when(step == 1)
                def _():
                    both_halves = part[...].astype(BF)
                    tp_s[0, 1, pl.ds(0, QUART)] = both_halves[0:QUART]
                    tp_s[1, 1, pl.ds(QUART, QUART)] = both_halves[QUART:HALF]
                    copy_rp(0, 1, True).start()
                    copy_rp(1, 1, True).start()

                @pl.when((step > 1) & (step < last))
                def _():
                    wait_rp(d, step - 1)
                    tp_s[d, step] = (part[...] + tp_r[d, step - 1].astype(F32)).astype(BF)
                    copy_rp(d, step, False).start()

                @pl.when(step == last)
                def _():
                    copy_rp(0, FAR, False).wait_recv()
                    copy_rp(1, FAR, False).wait_recv()
                    fs1[...] = (part[...] + tp_r[0, FAR].astype(F32) + tp_r[1, FAR].astype(F32)).astype(BF)

            @pl.when(((step == 1) & (d == 1)) | ((step == last) & (d == 0)) | ((step > 1) & (step < last)))
            def _():
                product(tblock(h, d, dist), HI)
                copy_rx(d, dist).wait_recv()
                summed = part[...] + xr[d, dist].astype(F32)

                @pl.when(step == 1)
                def _():
                    tb_s[1, 1] = summed.astype(BF)
                    copy_rb(1, 1).start()

                @pl.when((step > 1) & (step < last))
                def _():
                    @pl.when((step > 2) | (d == 1))
                    def _():
                        copy_rb(d, step - 1).wait_recv()

                    tb_s[d, step] = (summed + tb_r[d, step - 1].astype(F32)).astype(BF)
                    copy_rb(d, step).start()

                @pl.when(step == last)
                def _():
                    copy_rb(0, FAR).wait_recv()
                    copy_rb(1, FAR).wait_recv()
                    fs0[HI, :] = (summed + tb_r[0, FAR].astype(F32) + tb_r[1, FAR].astype(F32)).astype(BF)

            return carry2

        lax.fori_loop(0, 2, side, 0)
        router_stage(step)
        weight_grads(step)
        return carry

    lax.fori_loop(0, last + 1, scatter_step, 0)

    def ret_copy0(dq):
        qd = qwrap(q + dq)
        return rcopy(fs0.at[rows_of(qd)], ret0.at[rows_of(q)], r_ssem.at[dq], r_rsem.at[dq], dev(h, z, c, qd))

    def ret_land0(dq):
        land = ret0.at[rows_of(qwrap(q - dq))]
        return rcopy(land, land, r_ssem.at[dq], r_rsem.at[dq], sib)

    def ret_copy1(qd):
        return rcopy(fs1.at[rows_of(qd)], ret1.at[rows_of(q)], q_ssem.at[qd], q_rsem.at[q], dev(1 - h, z, c, qd))

    def ret_land1(i):
        land = ret1.at[rows_of(i)]
        return rcopy(land, land, q_ssem.at[0], q_rsem.at[i], sib)

    for qd in range(NE // 2):
        ret_copy1(qd).start()
    for dq in range(1, NE):
        ret_copy0(dq).start()
    ret0[rows_of(q), :] = fs0[rows_of(q), :]
    for dq in range(1, NE):
        ret_land0(dq).wait_recv()
    chosen = pick[...]
    got = dot_tn(chosen, ret0[...])

    @pl.when(q >= NE // 2)
    def _():
        outs[...] = got.astype(BF)

    @pl.when(q < NE // 2)
    def _():
        for i in range(NE):
            ret_land1(i).wait_recv()
        outs[...] = (got + dot_tn(chosen, ret1[...])).astype(BF)

    final = rcopy(outs, outr, o_sem.at[0], o_sem.at[1], sib)
    final.start()

    trade.wait_send()

    @pl.when(q < NE // 2)
    def _():
        for dq in range(NE):
            disp(1, dq).wait_send()

    for dq in range(1, NE):
        disp(0, dq).wait_send()
        ret_copy0(dq).wait_send()
    for qd in range(NE // 2):
        ret_copy1(qd).wait_send()

    def drain(k, carry):
        @pl.when(k >= 1)
        def _():
            copy_a(0, k).wait_send()
            copy_b(1, k).wait_send()

            @pl.when(k < FAR)
            def _():
                for d in range(2):
                    copy_p(d, k, False).wait_send()
                copy_a(1, k).wait_send()
                copy_b(0, k).wait_send()
                copy_f(0, k).wait_send()

            @pl.when(k == FAR)
            def _():
                for d in range(2):
                    copy_p(d, k, True).wait_send()

            copy_f(1, k).wait_send()
            copy_rx(1, k).wait_send()

            @pl.when(k < FAR)
            def _():
                copy_rx(0, k).wait_send()

            @pl.when(k == 1)
            def _():
                copy_ra(0, 1).wait_send()
                copy_rb(1, 1).wait_send()
                for d in range(2):
                    copy_rp(d, 1, True).wait_send()

            @pl.when(k > 1)
            def _():
                for d in range(2):
                    copy_ra(d, k).wait_send()
                    copy_rb(d, k).wait_send()
                    copy_rp(d, k, False).wait_send()

        @pl.when(k == 0)
        def _():
            copy_f(0, 0).wait_send()
            copy_rx(0, 0).wait_send()

        return carry

    lax.fori_loop(0, FAR + 1, drain, 0)
    middle.wait_send()

    @pl.when(c == 0)
    def _():
        w_in_give.wait_send()
        for dq in range(1, NE):
            meta_copy(dq).wait_send()
        for i, (dh, dq) in enumerate(plane):
            copy_g1(i, dh, dq).wait_send()
            copy_g3(i, dh, dq).wait_send()
        for dz in range(1, NZ):
            copy_g2(dz).wait_send()
        gr_ref[...] = g3[...]
        g4.wait_send()
        gu_own.wait()
        gu_give.wait_send()
        gd_give.wait_recv()

    @pl.when(c == 1)
    def _():
        w_out_give.wait_send()
        g4.wait_recv()
        gd_own.wait()
        gd_give.wait_send()
        gu_give.wait_recv()

    final.wait()

    @pl.when(c == 0)
    def _():
        og_ref[...] = outs[...]
        om_ref[...] = outr[...]

    @pl.when(c == 1)
    def _():
        og_ref[...] = outr[...]
        om_ref[...] = outs[...]


def vm(*shape, dtype=BF):
    return pltpu.VMEM(shape, dtype)


def dma(*shape):
    return pltpu.SemaphoreType.DMA(shape)


def shards(tokens, expert_ids, slot_ids, router, up_weight, down_weight, cotangent):
    core = lax.rem(lax.axis_index("section"), 2)
    first = core == 0
    keep = jnp.where(first, tokens, cotangent)
    give = jnp.where(first, cotangent, tokens)
    zero = jnp.zeros_like(tokens)

    def padded(v):
        return jnp.concatenate([jnp.where(first, v, zero), jnp.where(first, zero, v)], axis=1)

    vspec = pl.BlockSpec(memory_space=pltpu.VMEM)
    aspec = pl.BlockSpec(memory_space=pl.ANY)
    om, og, gu, gd, gr = pl.pallas_call(
        kernel,
        out_shape=(
            jax.ShapeDtypeStruct((TOK, BLK), BF),
            jax.ShapeDtypeStruct((TOK, BLK), BF),
            jax.ShapeDtypeStruct((WIDTH, HID), BF),
            jax.ShapeDtypeStruct((HID, WIDTH), BF),
            jax.ShapeDtypeStruct((NBLK, NE, BLK), F32),
        ),
        in_specs=[vspec, vspec, vspec, vspec, vspec, aspec, aspec],
        out_specs=(vspec, vspec, aspec, aspec, vspec),
        scratch_shapes=[
            vm(NBLK, ROWS, BLK), vm(2, WIDTH, HID), vm(2, HID, WIDTH), vm(2, WIDTH, HID), vm(2, HID, WIDTH),
            vm(128, WIDTH), vm(ROWS, TOK), vm(TOK, BLK), vm(ROWS, BLK), vm(ROWS, 128), vm(ROWS, 128),
            vm(ROWS, 2 * HID, dtype=F32), vm(ROWS, 128, dtype=F32), vm(ROWS, 2 * HID), vm(ROWS, 2 * HID),
            vm(ROWS, 2 * HID), vm(ROWS, 128), vm(ROWS, 128), vm(HALF, BLK, dtype=F32),
            vm(2, 5, HALF, BLK), vm(2, 5, HALF, BLK), vm(2, 5, HALF, BLK), vm(2, 5, HALF, BLK),
            vm(2, 5, HALF, BLK), vm(2, 5, HALF, BLK), vm(2, 5, HALF, BLK), vm(2, 5, HALF, BLK),
            vm(ROWS, BLK), vm(HALF, BLK), vm(ROWS, BLK), vm(ROWS, BLK), vm(TOK, BLK), vm(TOK, BLK),
            vm(NBLK, NE, BLK, dtype=F32), vm(15, NE, BLK, dtype=F32), vm(NE, BLK, dtype=F32),
            vm(NZ, NE, BLK, dtype=F32), vm(NE, BLK, dtype=F32), vm(NBLK, NE, BLK, dtype=F32),
            dma(3), dma(2), dma(2, NE), dma(2, NE), dma(NE), dma(NE),
            dma(2, 5), dma(2, 5), dma(2, 5), dma(2, 5), dma(2, 5), dma(2, 5), dma(2, 5), dma(2, 5),
            dma(2), dma(2, 5), dma(2, 5), dma(2, 5), dma(2, 5), dma(2, 5), dma(2, 5), dma(2, 5), dma(2, 5),
            dma(3), dma(NE), dma(NE), dma(NE), dma(NE), dma(2),
            dma(15), dma(15), dma(NZ), dma(NZ), dma(15), dma(15), dma(2),
        ],
        compiler_params=pltpu.CompilerParams(
            collective_id=0, has_side_effects=True, vmem_limit_bytes=60 << 20
        ),
    )(
        padded(keep), padded(give), expert_ids.T, slot_ids.T, router.T, up_weight[0], down_weight[0]
    )
    mixed = jnp.where(first, om[:, :FEAT], om[:, FEAT:])
    grad_tokens = jnp.where(first, og[:, :FEAT], og[:, FEAT:])
    grad_router = gr.transpose(0, 2, 1).reshape(WIDTH, NE)
    return (mixed, grad_tokens, gu[None], gd[None], grad_router)


def solution(mesh):
    in_specs = (
        P("expert", "section"),
        P("expert", None),
        P("expert", None),
        P(),
        P("expert", None, "section"),
        P("expert", "section", None),
        P("expert", "section"),
    )
    out_specs = (
        P("expert", "section"),
        P("expert", "section"),
        P("expert", None, "section"),
        P("expert", "section", None),
        P(),
    )
    return jax.shard_map(shards, mesh=mesh, in_specs=in_specs, out_specs=out_specs, check_vma=False)
```

time: 799 us -> 131 us (0.16)
  waiting for transfers between devices: 576 us -> 0 us
  blocking collectives: 131 us -> 0 us
  Pallas kernels: 0 us -> 119 us
  matrix products: 45.3 us -> 0 us
  starting transfers between devices: 13.5 us -> 0 us
  between operations: 14 us -> 0.65 us
  local copies, waits for them, and re-layouts: 15.4 us -> 6.25 us
    psum x1 -> x0, waiting for transfers between devices: 241 us -> none  [shards(): grad_router = lax.psum(placed_router, ('section', 'expert'))]
    reduce_scatter x2 -> x0, waiting for transfers between devices: 171 us -> none  [the longest x1 122 us: shards(): lax.psum_scatter(backward_part.astype(jnp.bfloat16), 'section', scatter_d...]
    pallas_call x0 -> x1, Pallas kernels: none -> 119 us  [shards(): pl.pallas_call(kernel, out_shape=(jax.ShapeDtypeStruct((TOK, BLK), BF), j...]
    all_gather x2 -> x0, waiting for transfers between devices: 110 us -> none  [the longest x1 88.7 us: shards(): lax.all_gather(tokens, 'section', axis=1, tiled=True)]
    psum x1 -> x0, blocking collectives: 70.1 us -> none  [shards(): lax.psum((jnp.sum(cot_float * out_first, axis=1), jnp.sum(cot_float * out...]
    all_to_all x1 -> x0, blocking collectives: 61.3 us -> none  [shards(): lax.all_to_all(sent_cot.reshape(block_shape), 'expert', split_axis=0, con...]
    all_to_all x3 -> x0, waiting for transfers between devices: 53.5 us -> none  [the longest x1 53.5 us: shards(): lax.all_to_all(sent_in.reshape(block_shape), 'expert', split_axis=0, conc...]
    dot_general x15 -> x0, matrix products: 45.3 us -> none  [the longest x1 5.89 us: shards(): lax.dot_general(rows_in, pre_grad, (((0,), (0,)), ((), ())), preferred_el...]
  transfers between devices with their start and end apart: 8 -> 0, of which waited for: 6 -> 0; matrix products, arithmetic and copies ran while one was open for 6% -> 0% of each run, Pallas kernels for 0% -> 0%
where the time goes in v1:
time: 131 us
  Pallas kernels  119 us (91%)
  local copies, waits for them, and re-layouts  6.25 us (5%)
  other arithmetic  4.33 us (3%)
    pallas_call x1, Pallas kernels, shards(): pl.pallas_call(kernel, out_shape=(jax.ShapeDtypeStruct((TOK, BLK), BF), j...  119 us
    unnamed x7, local copies, waits for them, and re-layouts  6.25 us

profile of v1, /device:TPU:1, one launch (start us, length us, event | category | flops | bytes accessed | tf_op | source)
XLA Modules:
  0.0 130.6 jit_solution(9792633492492929658)
XLA Ops:
  0.6 1.0 broadcast_select_fusion.1
  1.6 0.8 pad_maximum_fusion.1.give_ref
  2.4 0.8 pad_maximum_fusion.keep_ref
  3.1 119.4 %shard_map.110 = (bf16[192,384]{1,0:T(8,128)(2,1)}, bf16[192,384]{1,0:T(8,128)(2,1)}, bf16[6144,256]{1,0:T(8,128)(2,1)}, bf16[256,6144]{1,0:T(8,128)(2,1)}, f32[16,8,384]{2,1,0:T(8,128)}) custom-call(bf16[192,384]{1,0:T(8,128)(2,1)} %pad_maximum_fusion.keep_ref, bf16[192,384]{1,0:T(8,128)(2,1)} %pad_maximum_fusion.1.give_ref, s32[2,192]{1,0:T(2,128)} %bitcast.16, ...), custom_call_target="tpu_custom_call" | custom-call | tf_op jit(solution)/shard_map/pallas_call | solution.py:773
  122.5 1.8 %slice_select_fusion = (bf16[192,192]{1,0:T(8,128)(2,1)}, bf16[192,192]{1,0:T(8,128)(2,1)}) fusion(bf16[192,384]{1,0:T(8,128)(2,1)} %get-tuple-element.11, pred[]{:T(512)S(6)} %eq.3, bf16[192,384]{1,0:T(8,128)(2,1)} %get-tuple-element.10), kind=kLoop, calls=%fused_computation.2 | loop fusion | flops 73728 | bytes 442369 | tf_op jit(solution)/shard_map/jit(_where)/select_n | solution.py:807
  124.3 0.0 copy-start
  124.3 3.9 %copy.15 = bf16[1,6144,256]{2,1,0:T(8,128)(2,1)} copy(bf16[1,6144,256]{2,1,0:T(8,128)(2,1)} %bitcast.13) | data formatting | bytes 6291456
  128.2 0.0 copy-done
  128.2 0.0 copy-start.1
  128.2 1.7 %copy.16 = bf16[1,256,6144]{2,1,0:T(8,128)(2,1)} copy(bf16[1,256,6144]{2,1,0:T(8,128)(2,1)S(1)} %bitcast.12) | data formatting | bytes 6291456
  129.9 0.0 copy-done.1
  129.9 0.7 copy.17
Async XLA Ops:
  124.3 3.9 %copy-start = (bf16[256,6144]{1,0:T(8,128)(2,1)S(1)}, bf16[256,6144]{1,0:T(8,128)(2,1)}, u32[]{:S(2)}) copy-start(bf16[256,6144]{1,0:T(8,128)(2,1)} %get-tuple-element.13) | copy-start | bytes 9437188
  128.2 1.7 %copy-start.1 = (f32[16,8,384]{2,1,0:T(8,128)S(1)}, f32[16,8,384]{2,1,0:T(8,128)}, u32[]{:S(2)}) copy-start(f32[16,8,384]{2,1,0:T(8,128)} %get-tuple-element.14) | copy-start | bytes 589828

commit v2 on v1

--- a/solution.py
+++ b/solution.py
@@ -46,14 +46,14 @@
 
 
 def kernel(
-    keep_ref, give_ref, ids_ref, slots_ref, rt_ref, up_ref, dn_ref,
+    tok_ref, cot_ref, ids_hbm, slots_hbm, rt_hbm, up_ref, dn_ref,
     om_ref, og_ref, gu_ref, gd_ref, gr_ref,
-    gath, wu, wd, gu, gd, rt3, pick, xch, sent, msend, meta,
+    gath, wu, wd, gu, gd, rt3, pick, keep, give, ids_ref, slots_ref, rt_ref, xch, sent, msend, meta,
     pre, logit, ms, mr, pg, tsb, tlb, part,
     ta_s, ta_r, tb_s, tb_r, tp_s, tp_r, xs, xr,
-    fs0, fs1, ret0, ret1, outs, outr,
+    fs0, fs1, ret0, ret1, outs, outo, outr,
     gp, g1, g2s, g2, g3s, g3,
-    w_sem, x_sem, d_ssem, d_rsem, m_ssem, m_rsem,
+    in_sem, w_sem, x_sem, d_ssem, d_rsem, m_ssem, m_rsem,
     a_ssem, a_rsem, b_ssem, b_rsem, p_ssem, p_rsem, f_ssem, f_rsem,
     mid_sem, ra_ssem, ra_rsem, rb_ssem, rb_rsem, rp_ssem, rp_rsem, rx_ssem, rx_rsem,
     gsem, r_ssem, r_rsem, q_ssem, q_rsem, o_sem,
@@ -96,11 +96,18 @@
         peers.append(dev(h, zwrap(z + dz), c, q))
     for peer in peers:
         pl.semaphore_signal(barrier, inc=1, device_id=peer, device_id_type=MESH)
-    pl.semaphore_wait(barrier, len(peers))
-
-    trade = rcopy(give_ref, xch, x_sem.at[0], x_sem.at[1], sib)
-    trade.start()
-
+
+    small = [
+        pltpu.make_async_copy(ids_hbm, ids_ref, in_sem.at[0]),
+        pltpu.make_async_copy(slots_hbm, slots_ref, in_sem.at[1]),
+        pltpu.make_async_copy(rt_hbm, rt_ref, in_sem.at[2]),
+    ]
+    for copy in small:
+        copy.start()
+    tok_keep = pltpu.make_async_copy(tok_ref, keep, in_sem.at[3])
+    cot_give = pltpu.make_async_copy(cot_ref, give, in_sem.at[4])
+    cot_keep = pltpu.make_async_copy(cot_ref, keep, in_sem.at[3])
+    tok_give = pltpu.make_async_copy(tok_ref, give, in_sem.at[4])
     w_in = pltpu.make_async_copy(up_ref, wu.at[0], w_sem.at[0])
     w_in_give = rcopy(dn_ref, wd.at[0], w_sem.at[1], w_sem.at[2], sib)
     w_out = pltpu.make_async_copy(dn_ref, wd.at[1], w_sem.at[0])
@@ -108,13 +115,18 @@
 
     @pl.when(c == 0)
     def _():
+        cot_give.start()
+        tok_keep.start()
         w_in.start()
-        w_in_give.start()
 
     @pl.when(c == 1)
     def _():
+        tok_give.start()
+        cot_keep.start()
         w_out.start()
-        w_out_give.start()
+
+    small[0].wait()
+    small[1].wait()
 
     place0 = ids_ref[0:1, :] * CAP + slots_ref[0:1, :]
     place1 = ids_ref[1:2, :] * CAP + slots_ref[1:2, :]
@@ -140,8 +152,27 @@
     pre[...] = jnp.zeros((ROWS, 2 * HID), F32)
     logit[...] = jnp.zeros((ROWS, 128), F32)
 
+    row = lax.broadcasted_iota(jnp.int32, (FEAT, BLK), 0)
+    col = lax.broadcasted_iota(jnp.int32, (FEAT, BLK), 1)
+    place_mine = (col == row + FEAT * c).astype(F32).astype(BF)
+    place_other = (col == row + FEAT * (1 - c)).astype(F32).astype(BF)
+
+    @pl.when(c == 0)
+    def _():
+        cot_give.wait()
+        tok_keep.wait()
+
+    @pl.when(c == 1)
+    def _():
+        tok_give.wait()
+        cot_keep.wait()
+
+    pl.semaphore_wait(barrier, len(peers))
+    trade = rcopy(give, xch, x_sem.at[0], x_sem.at[1], sib)
+    trade.start()
+    half_both = dot_nn(keep[...], place_mine)
     trade.wait_recv()
-    both = keep_ref[...] + xch[...]
+    both = (half_both + dot_nn(xch[...], place_other)).astype(BF)
     sent[...] = dot_nn(pick[...], both).astype(BF)
 
     mine = h * NZ + z
@@ -167,21 +198,28 @@
         land = meta.at[rows_of(qwrap(q - dq))]
         return rcopy(land, land, m_ssem.at[dq], m_rsem.at[dq], sib)
 
+    for dq in range(1, NE):
+        disp(0, dq).start()
+
     @pl.when(q < NE // 2)
     def _():
         for dq in range(NE):
             disp(1, dq).start()
 
-    for dq in range(1, NE):
-        disp(0, dq).start()
+    gath[mine, rows_of(q), :] = sent[rows_of(q), :]
 
     @pl.when(c == 0)
     def _():
+        w_in_give.start()
         for dq in range(1, NE):
             meta_copy(dq).start()
         meta[rows_of(q), :] = msend[rows_of(q), :]
 
-    gath[mine, rows_of(q), :] = sent[rows_of(q), :]
+    @pl.when(c == 1)
+    def _():
+        w_out_give.start()
+
+    small[2].wait()
 
     def zblock(hh, d, k):
         return hh * NZ + zwrap(z - k + 2 * d * k)
@@ -436,7 +474,7 @@
         hh, qq = lax.rem(h + dh, 2), qwrap(q - dq)
         return rcopy(g3s, g3.at[hh * NE + qq], g3_ssem.at[i], g3_rsem.at[i], sib)
 
-    g4 = rcopy(g3, gr_ref, g4_sem.at[0], g4_sem.at[1], sib)
+    g4 = rcopy(g3, g3, g4_sem.at[0], g4_sem.at[1], sib)
 
     def router_stage(step):
         @pl.when((c == 0) & (step == 0))
@@ -479,10 +517,8 @@
                 land_g3(i, dh, dq).wait_recv()
             g4.start()
 
-    gu_own = pltpu.make_async_copy(gu.at[0], gu_ref, gsem.at[0])
-    gu_give = rcopy(gu.at[1], gu_ref, gsem.at[1], gsem.at[2], sib)
-    gd_own = pltpu.make_async_copy(gd.at[1], gd_ref, gsem.at[0])
-    gd_give = rcopy(gd.at[0], gd_ref, gsem.at[1], gsem.at[2], sib)
+    gu_give = rcopy(gu, gu_ref, gsem.at[1], gsem.at[2], sib)
+    gd_give = rcopy(gd, gd_ref, gsem.at[1], gsem.at[2], sib)
 
     def weight_grads(step):
         def one(i, carry):
@@ -491,14 +527,14 @@
             @pl.when(c == 0)
             def _():
                 full = dot_tn(gath[p], pg[...]).astype(BF)
-                gu[0, lanes(p), :] = full[:, 0:HID]
-                gu[1, lanes(p), :] = full[:, HID : 2 * HID]
+                gu_ref[lanes(p), :] = full[:, 0:HID]
+                gu[lanes(p), :] = full[:, HID : 2 * HID]
 
             @pl.when(c == 1)
             def _():
                 full = dot_tn(mr[...], gath[p]).astype(BF)
-                gd[0, :, lanes(p)] = full[0:HID]
-                gd[1, :, lanes(p)] = full[HID : 2 * HID]
+                gd[:, lanes(p)] = full[0:HID]
+                gd_ref[:, lanes(p)] = full[HID : 2 * HID]
 
             return carry
 
@@ -508,13 +544,26 @@
 
         @pl.when((step == 3) & (c == 0))
         def _():
-            gu_own.start()
             gu_give.start()
 
         @pl.when((step == 3) & (c == 1))
         def _():
-            gd_own.start()
             gd_give.start()
+
+    def ret_copy0(dq):
+        qd = qwrap(q + dq)
+        return rcopy(fs0.at[rows_of(qd)], ret0.at[rows_of(q)], r_ssem.at[dq], r_rsem.at[dq], dev(h, z, c, qd))
+
+    def ret_land0(dq):
+        land = ret0.at[rows_of(qwrap(q - dq))]
+        return rcopy(land, land, r_ssem.at[dq], r_rsem.at[dq], sib)
+
+    def ret_copy1(qd):
+        return rcopy(fs1.at[rows_of(qd)], ret1.at[rows_of(q)], q_ssem.at[qd], q_rsem.at[q], dev(1 - h, z, c, qd))
+
+    def ret_land1(i):
+        land = ret1.at[rows_of(i)]
+        return rcopy(land, land, q_ssem.at[0], q_rsem.at[i], sib)
 
     last = FAR + 1
 
@@ -522,13 +571,18 @@
         dist = last - step
         nxt = FAR - step
 
-        def side(d, carry2):
+        def share(d, carry2):
             @pl.when(((step == 0) & (d == 1)) | ((step >= 1) & (step < FAR)) | ((step == FAR) & (d == 0)))
             def _():
                 product(tblock(1 - h, d, nxt), HI)
                 xs[d, nxt] = part[...].astype(BF)
                 copy_rx(d, nxt).start()
 
+            return carry2
+
+        lax.fori_loop(0, 2, share, 0)
+
+        def own_first(d, carry2):
             @pl.when((((step == 1) | (step == last)) & (d == 0)) | ((step > 1) & (step < last)))
             def _():
                 product(tblock(h, d, dist), LO)
@@ -552,7 +606,20 @@
                     copy_ra(0, FAR).wait_recv()
                     copy_ra(1, FAR).wait_recv()
                     fs0[LO, :] = (part[...] + ta_r[0, FAR].astype(F32) + ta_r[1, FAR].astype(F32)).astype(BF)
-
+                    for dq in range(NE):
+
+                        @pl.when(qwrap(q + dq) < NE // 2)
+                        def _():
+                            if dq:
+                                ret_copy0(dq).start()
+                            else:
+                                ret0[rows_of(q), :] = fs0[rows_of(q), :]
+
+            return carry2
+
+        lax.fori_loop(0, 2, own_first, 0)
+
+        def other_first(d, carry2):
             @pl.when((((step == 1) | (step == last)) & (d == 0)) | ((step > 1) & (step < last)))
             def _():
                 product(tblock(1 - h, d, dist), LO)
@@ -576,7 +643,14 @@
                     copy_rp(0, FAR, False).wait_recv()
                     copy_rp(1, FAR, False).wait_recv()
                     fs1[...] = (part[...] + tp_r[0, FAR].astype(F32) + tp_r[1, FAR].astype(F32)).astype(BF)
-
+                    for qd in range(NE // 2):
+                        ret_copy1(qd).start()
+
+            return carry2
+
+        lax.fori_loop(0, 2, other_first, 0)
+
+        def own_second(d, carry2):
             @pl.when(((step == 1) & (d == 1)) | ((step == last) & (d == 0)) | ((step > 1) & (step < last)))
             def _():
                 product(tblock(h, d, dist), HI)
@@ -602,53 +676,46 @@
                     copy_rb(0, FAR).wait_recv()
                     copy_rb(1, FAR).wait_recv()
                     fs0[HI, :] = (summed + tb_r[0, FAR].astype(F32) + tb_r[1, FAR].astype(F32)).astype(BF)
+                    for dq in range(NE):
+
+                        @pl.when(qwrap(q + dq) >= NE // 2)
+                        def _():
+                            if dq:
+                                ret_copy0(dq).start()
+                            else:
+                                ret0[rows_of(q), :] = fs0[rows_of(q), :]
 
             return carry2
 
-        lax.fori_loop(0, 2, side, 0)
+        lax.fori_loop(0, 2, own_second, 0)
         router_stage(step)
         weight_grads(step)
         return carry
 
     lax.fori_loop(0, last + 1, scatter_step, 0)
 
-    def ret_copy0(dq):
-        qd = qwrap(q + dq)
-        return rcopy(fs0.at[rows_of(qd)], ret0.at[rows_of(q)], r_ssem.at[dq], r_rsem.at[dq], dev(h, z, c, qd))
-
-    def ret_land0(dq):
-        land = ret0.at[rows_of(qwrap(q - dq))]
-        return rcopy(land, land, r_ssem.at[dq], r_rsem.at[dq], sib)
-
-    def ret_copy1(qd):
-        return rcopy(fs1.at[rows_of(qd)], ret1.at[rows_of(q)], q_ssem.at[qd], q_rsem.at[q], dev(1 - h, z, c, qd))
-
-    def ret_land1(i):
-        land = ret1.at[rows_of(i)]
-        return rcopy(land, land, q_ssem.at[0], q_rsem.at[i], sib)
-
-    for qd in range(NE // 2):
-        ret_copy1(qd).start()
-    for dq in range(1, NE):
-        ret_copy0(dq).start()
-    ret0[rows_of(q), :] = fs0[rows_of(q), :]
     for dq in range(1, NE):
         ret_land0(dq).wait_recv()
     chosen = pick[...]
     got = dot_tn(chosen, ret0[...])
 
+    def give_out(total):
+        rounded = total.astype(BF)
+        outo[...] = dot_nt(rounded, place_other).astype(BF)
+        final.start()
+        outs[...] = dot_nt(rounded, place_mine).astype(BF)
+
+    final = rcopy(outo, outr, o_sem.at[0], o_sem.at[1], sib)
+
     @pl.when(q >= NE // 2)
     def _():
-        outs[...] = got.astype(BF)
+        give_out(got)
 
     @pl.when(q < NE // 2)
     def _():
         for i in range(NE):
             ret_land1(i).wait_recv()
-        outs[...] = (got + dot_tn(chosen, ret1[...])).astype(BF)
-
-    final = rcopy(outs, outr, o_sem.at[0], o_sem.at[1], sib)
-    final.start()
+        give_out(got + dot_tn(chosen, ret1[...]))
 
     trade.wait_send()
 
@@ -723,9 +790,7 @@
             copy_g3(i, dh, dq).wait_send()
         for dz in range(1, NZ):
             copy_g2(dz).wait_send()
-        gr_ref[...] = g3[...]
         g4.wait_send()
-        gu_own.wait()
         gu_give.wait_send()
         gd_give.wait_recv()
 
@@ -733,10 +798,11 @@
     def _():
         w_out_give.wait_send()
         g4.wait_recv()
-        gd_own.wait()
         gd_give.wait_send()
         gu_give.wait_recv()
 
+    for p in range(NBLK):
+        gr_ref[:, p * BLK : (p + 1) * BLK] = g3[p]
     final.wait()
 
     @pl.when(c == 0)
@@ -758,55 +824,71 @@
     return pltpu.SemaphoreType.DMA(shape)
 
 
+def store(om, og, gu, gd, gr, om_out, og_out, gu_out, gd_out, gr_out, sem):
+    copies = [
+        pltpu.make_async_copy(src, dst, sem.at[i])
+        for i, (src, dst) in enumerate(((gu, gu_out), (gd, gd_out), (om, om_out), (og, og_out), (gr, gr_out)))
+    ]
+    for copy in copies:
+        copy.start()
+    for copy in copies:
+        copy.wait()
+
+
 def shards(tokens, expert_ids, slot_ids, router, up_weight, down_weight, cotangent):
-    core = lax.rem(lax.axis_index("section"), 2)
-    first = core == 0
-    keep = jnp.where(first, tokens, cotangent)
-    give = jnp.where(first, cotangent, tokens)
-    zero = jnp.zeros_like(tokens)
-
-    def padded(v):
-        return jnp.concatenate([jnp.where(first, v, zero), jnp.where(first, zero, v)], axis=1)
-
     vspec = pl.BlockSpec(memory_space=pltpu.VMEM)
     aspec = pl.BlockSpec(memory_space=pl.ANY)
-    om, og, gu, gd, gr = pl.pallas_call(
+    hspec = pl.BlockSpec(memory_space=pltpu.HBM)
+    shapes = (
+        jax.ShapeDtypeStruct((TOK, FEAT), BF),
+        jax.ShapeDtypeStruct((TOK, FEAT), BF),
+        jax.ShapeDtypeStruct((WIDTH, HID), BF),
+        jax.ShapeDtypeStruct((HID, WIDTH), BF),
+        jax.ShapeDtypeStruct((NE, WIDTH), F32),
+    )
+    results = pl.pallas_call(
         kernel,
         out_shape=(
-            jax.ShapeDtypeStruct((TOK, BLK), BF),
-            jax.ShapeDtypeStruct((TOK, BLK), BF),
-            jax.ShapeDtypeStruct((WIDTH, HID), BF),
-            jax.ShapeDtypeStruct((HID, WIDTH), BF),
-            jax.ShapeDtypeStruct((NBLK, NE, BLK), F32),
+            *shapes,
         ),
-        in_specs=[vspec, vspec, vspec, vspec, vspec, aspec, aspec],
-        out_specs=(vspec, vspec, aspec, aspec, vspec),
+        in_specs=[hspec] * 7,
+        out_specs=(vspec,) * 5,
         scratch_shapes=[
-            vm(NBLK, ROWS, BLK), vm(2, WIDTH, HID), vm(2, HID, WIDTH), vm(2, WIDTH, HID), vm(2, HID, WIDTH),
-            vm(128, WIDTH), vm(ROWS, TOK), vm(TOK, BLK), vm(ROWS, BLK), vm(ROWS, 128), vm(ROWS, 128),
+            vm(NBLK, ROWS, BLK), vm(2, WIDTH, HID), vm(2, HID, WIDTH), vm(WIDTH, HID), vm(HID, WIDTH),
+            vm(128, WIDTH), vm(ROWS, TOK), vm(TOK, FEAT), vm(TOK, FEAT),
+            vm(2, TOK, dtype=jnp.int32), vm(2, TOK, dtype=jnp.int32), vm(NE, WIDTH, dtype=F32),
+            vm(TOK, FEAT), vm(ROWS, BLK), vm(ROWS, 128), vm(ROWS, 128),
             vm(ROWS, 2 * HID, dtype=F32), vm(ROWS, 128, dtype=F32), vm(ROWS, 2 * HID), vm(ROWS, 2 * HID),
             vm(ROWS, 2 * HID), vm(ROWS, 128), vm(ROWS, 128), vm(HALF, BLK, dtype=F32),
             vm(2, 5, HALF, BLK), vm(2, 5, HALF, BLK), vm(2, 5, HALF, BLK), vm(2, 5, HALF, BLK),
             vm(2, 5, HALF, BLK), vm(2, 5, HALF, BLK), vm(2, 5, HALF, BLK), vm(2, 5, HALF, BLK),
-            vm(ROWS, BLK), vm(HALF, BLK), vm(ROWS, BLK), vm(ROWS, BLK), vm(TOK, BLK), vm(TOK, BLK),
+            vm(ROWS, BLK), vm(HALF, BLK), vm(ROWS, BLK), vm(ROWS, BLK), vm(TOK, FEAT), vm(TOK, FEAT), vm(TOK, FEAT),
             vm(NBLK, NE, BLK, dtype=F32), vm(15, NE, BLK, dtype=F32), vm(NE, BLK, dtype=F32),
             vm(NZ, NE, BLK, dtype=F32), vm(NE, BLK, dtype=F32), vm(NBLK, NE, BLK, dtype=F32),
-            dma(3), dma(2), dma(2, NE), dma(2, NE), dma(NE), dma(NE),
+            dma(5), dma(3), dma(2), dma(2, NE), dma(2, NE), dma(NE), dma(NE),
             dma(2, 5), dma(2, 5), dma(2, 5), dma(2, 5), dma(2, 5), dma(2, 5), dma(2, 5), dma(2, 5),
             dma(2), dma(2, 5), dma(2, 5), dma(2, 5), dma(2, 5), dma(2, 5), dma(2, 5), dma(2, 5), dma(2, 5),
             dma(3), dma(NE), dma(NE), dma(NE), dma(NE), dma(2),
             dma(15), dma(15), dma(NZ), dma(NZ), dma(15), dma(15), dma(2),
         ],
         compiler_params=pltpu.CompilerParams(
-            collective_id=0, has_side_effects=True, vmem_limit_bytes=60 << 20
+            collective_id=0, has_side_effects=True, vmem_limit_bytes=44 << 20
         ),
     )(
-        padded(keep), padded(give), expert_ids.T, slot_ids.T, router.T, up_weight[0], down_weight[0]
+        *(
+            pltpu.with_memory_space_constraint(v, pltpu.HBM)
+            for v in (tokens, cotangent, expert_ids.T, slot_ids.T, router.T, up_weight[0], down_weight[0])
+        )
     )
-    mixed = jnp.where(first, om[:, :FEAT], om[:, FEAT:])
-    grad_tokens = jnp.where(first, og[:, :FEAT], og[:, FEAT:])
-    grad_router = gr.transpose(0, 2, 1).reshape(WIDTH, NE)
-    return (mixed, grad_tokens, gu[None], gd[None], grad_router)
+    mixed, grad_tokens, gu, gd, gr = pl.pallas_call(
+        store,
+        out_shape=shapes,
+        in_specs=[aspec] * 5,
+        out_specs=(hspec,) * 5,
+        scratch_shapes=[dma(5)],
+        compiler_params=pltpu.CompilerParams(vmem_limit_bytes=1 << 20),
+    )(*results)
+    return (mixed, grad_tokens, gu[None], gd[None], gr.T)
 
 
 def solution(mesh):

time: 131 us -> 116 us (0.89)
  local copies, waits for them, and re-layouts: 6.25 us -> 0 us
  other arithmetic: 4.33 us -> 0 us
  Pallas kernels: 119 us -> 115 us
    unnamed x7 -> x0, local copies, waits for them, and re-layouts: 6.25 us -> none
    pallas_call x1 -> x2, Pallas kernels: 119 us -> 115 us  [the longest x1 112 us: shards(): pl.pallas_call(kernel, out_shape=(*shapes,), in_specs=[hspec] * 7, out_sp...]
    select_n x2 -> x0, other arithmetic: 2.81 us -> none  [the longest x1 1.84 us: shards(): grad_tokens = jnp.where(first, og[:, :FEAT], og[:, FEAT:])]
    concatenate x2 -> x0, other arithmetic: 1.52 us -> none  [padded(): jnp.concatenate([jnp.where(first, v, zero), jnp.where(first, zero, v)], a...]
where the time goes in v2:
time: 116 us
  Pallas kernels  115 us (99%)
    pallas_call x1, Pallas kernels, shards(): pl.pallas_call(kernel, out_shape=(*shapes,), in_specs=[hspec] * 7, out_sp...  112 us
    pallas_call x1, Pallas kernels, shards(): pl.pallas_call(store, out_shape=shapes, in_specs=[aspec] * 5, out_specs=(...  2.85 us

profile of v2, /device:TPU:1, one launch (start us, length us, event | category | flops | bytes accessed | tf_op | source)
XLA Modules:
  0.0 115.6 jit_solution(10797101898557684491)
XLA Ops:
  0.6 112.1 %shard_map.110 = (bf16[192,192]{1,0:T(8,128)(2,1)S(1)}, bf16[192,192]{1,0:T(8,128)(2,1)S(1)}, bf16[6144,256]{1,0:T(8,128)(2,1)S(1)}, bf16[256,6144]{1,0:T(8,128)(2,1)S(1)}, f32[8,6144]{1,0:T(8,128)S(1)}) custom-call(bf16[192,192]{1,0:T(8,128)(2,1)} %tok_ref.1, bf16[192,192]{1,0:T(8,128)(2,1)} %cot_ref.1, s32[2,192]{1,0:T(2,128)} %bitcast.11, ...), custom_call_target="tpu_custom_call" | custom-call | tf_op jit(solution)/shard_map/pallas_call | solution.py:849
  112.7 2.9 %shard_map.111 = (bf16[192,192]{1,0:T(8,128)(2,1)}, bf16[192,192]{1,0:T(8,128)(2,1)}, bf16[6144,256]{1,0:T(8,128)(2,1)}, bf16[256,6144]{1,0:T(8,128)(2,1)}, f32[8,6144]{1,0:T(8,128)}) custom-call(bf16[192,192]{1,0:T(8,128)(2,1)S(1)} %get-tuple-element.15.om, bf16[192,192]{1,0:T(8,128)(2,1)S(1)} %get-tuple-element.16.og, ...), custom_call_target="tpu_custom_call" | custom-call | tf_op jit(solution)/shard_map/pallas_call | solution.py:883

commit v3 on v2

v3 whole, which is shorter than its diff:
```python
import jax
import jax.numpy as jnp
from jax import lax
from jax.experimental import pallas as pl
from jax.experimental.pallas import tpu as pltpu
from jax.sharding import PartitionSpec as P

MESH = pl.DeviceIdType.MESH
NZ = 8
FAR = NZ // 2
NE = 8
CAP = 48
TOK = 192
FEAT = 192
BLK = 2 * FEAT
ROWS = NE * CAP
HALF = ROWS // 2
QUART = HALF // 2
HID = 256
WIDTH = 6144
NBLK = WIDTH // BLK
BF = jnp.bfloat16
F32 = jnp.float32
NY = NE // 2


def dot_nn(a, b):
    return jnp.dot(a, b, preferred_element_type=F32)


def dot_nt(a, b):
    return lax.dot_general(a, b, (((1,), (1,)), ((), ())), preferred_element_type=F32)


def dot_tn(a, b):
    return lax.dot_general(a, b, (((0,), (0,)), ((), ())), preferred_element_type=F32)


def lanes(p):
    return pl.ds(pl.multiple_of(p * BLK, BLK), BLK)


def rows_of(q):
    return pl.ds(pl.multiple_of(q * CAP, CAP), CAP)


def kernel(
    tok_ref, cot_ref, ids_hbm, slots_hbm, rt_hbm, up_ref, dn_ref,
    om_ref, og_ref, gu_ref, gd_ref, gr_ref,
    gath, wu, wd, gu, gd, gu0, gd0, rt3, pick, keep, give, ids_ref, slots_ref, rt_ref, xch, sent, msend, meta,
    pre, logit, ms, mr, pg, tsb, tlb, part,
    ring_s, ring_r, xs, xr,
    fs0, fs1, ret0, ret1,
    gp, g1, g2s, g2, g3s, g3,
    in_sem, w_sem, x_sem, d_ssem, d_rsem, m_ssem, m_rsem,
    ag_ssem, ag_rsem, f_ssem, f_rsem, mid_sem, rs_ssem, rs_rsem, rx_ssem, rx_rsem,
    gsem, r_ssem, r_rsem, o_sem,
    g1_ssem, g1_rsem, g2_ssem, g2_rsem, g3_ssem, g3_rsem, g4_sem,
):
    s = lax.axis_index("section")
    q = lax.axis_index("expert")
    c = lax.rem(s, 2)
    z = lax.rem(s // 2, NZ)
    h = s // (2 * NZ)

    def dev(hh, zz, cc, qq):
        return ((hh * NZ + zz) * 2 + cc, qq)

    def zwrap(v):
        return lax.rem(v + 2 * NZ, NZ)

    def qwrap(v):
        return lax.rem(v + NE, NE)

    lo_x = q // NY
    y = lax.rem(q, NY)

    def first(off=0, size=HALF):
        return pl.ds(pl.multiple_of((1 - lo_x) * HALF + off, QUART), size)

    def second(off=0, size=HALF):
        return pl.ds(pl.multiple_of(lo_x * HALF + off, QUART), size)

    def group(same, dy):
        return (lo_x if same else 1 - lo_x) * NY + lax.rem(y + NY + dy, NY)

    sib = dev(h, z, 1 - c, q)
    partner = dev(1 - h, z, c, q)

    def znext(d):
        return dev(h, zwrap(z + 1 - 2 * d), c, q)

    def rcopy(src, dst, ssem, rsem, target):
        return pltpu.make_async_remote_copy(
            src_ref=src, dst_ref=dst, send_sem=ssem, recv_sem=rsem, device_id=target, device_id_type=MESH
        )

    barrier = pltpu.get_barrier_semaphore()
    peers = [sib]
    for dh in range(2):
        for dq in range(NE):
            if dh or dq:
                peers.append(dev(lax.rem(h + dh, 2), z, c, qwrap(q + dq)))
    for dz in range(1, NZ):
        peers.append(dev(h, zwrap(z + dz), c, q))
    for peer in peers:
        pl.semaphore_signal(barrier, inc=1, device_id=peer, device_id_type=MESH)

    small = [
        pltpu.make_async_copy(ids_hbm, ids_ref, in_sem.at[0]),
        pltpu.make_async_copy(slots_hbm, slots_ref, in_sem.at[1]),
        pltpu.make_async_copy(rt_hbm, rt_ref, in_sem.at[2]),
    ]
    for copy in small:
        copy.start()
    tok_keep = pltpu.make_async_copy(tok_ref, keep, in_sem.at[3])
    cot_give = pltpu.make_async_copy(cot_ref, give, in_sem.at[4])
    cot_keep = pltpu.make_async_copy(cot_ref, keep, in_sem.at[3])
    tok_give = pltpu.make_async_copy(tok_ref, give, in_sem.at[4])
    w_in = pltpu.make_async_copy(up_ref, wu.at[0], w_sem.at[0])
    w_in_give = rcopy(dn_ref, wd.at[0], w_sem.at[1], w_sem.at[2], sib)
    w_out = pltpu.make_async_copy(dn_ref, wd.at[1], w_sem.at[0])
    w_out_give = rcopy(up_ref, wu.at[1], w_sem.at[1], w_sem.at[2], sib)

    @pl.when(c == 0)
    def _():
        cot_give.start()
        tok_keep.start()
        w_in.start()

    @pl.when(c == 1)
    def _():
        tok_give.start()
        cot_keep.start()
        w_out.start()

    @pl.when(c == 0)
    def _():
        cot_give.wait()
        tok_keep.wait()

    @pl.when(c == 1)
    def _():
        tok_give.wait()
        cot_keep.wait()

    pl.semaphore_wait(barrier, len(peers))
    trade = rcopy(give, xch, x_sem.at[0], x_sem.at[1], sib)
    trade.start()
    row = lax.broadcasted_iota(jnp.int32, (FEAT, BLK), 0)
    col = lax.broadcasted_iota(jnp.int32, (FEAT, BLK), 1)
    place_mine = (col == row + FEAT * c).astype(F32).astype(BF)
    place_other = (col == row + FEAT * (1 - c)).astype(F32).astype(BF)

    small[0].wait()
    small[1].wait()

    place0 = ids_ref[0:1, :] * CAP + slots_ref[0:1, :]
    place1 = ids_ref[1:2, :] * CAP + slots_ref[1:2, :]
    slot = lax.broadcasted_iota(jnp.int32, (ROWS, TOK), 0)
    hit0 = (slot == place0).astype(F32)
    hit1 = (slot == place1).astype(F32)
    pick[...] = (hit0 + hit1).astype(BF)
    half_both = dot_nn(keep[...], place_mine)
    trade.wait_recv()
    both = (half_both + dot_nn(xch[...], place_other)).astype(BF)
    sent[...] = dot_nn(pick[...], both).astype(BF)

    mine = h * NZ + z

    def disp(kind, dy):
        qd = group(kind == 0, dy)
        return rcopy(
            sent.at[rows_of(qd)], gath.at[mine, rows_of(q)], d_ssem.at[kind], d_rsem.at[kind],
            dev(1 - h if kind == 2 else h, z, c, qd),
        )

    def rows_in(ref, kind):
        return ref.at[pl.ds(0, (NY - 1 if kind == 0 else NY) * CAP)]

    def disp_all(kind):
        ref = rows_in(sent, kind)
        return rcopy(ref, ref, d_ssem.at[kind], d_rsem.at[kind], sib)

    def meta_copy(dq):
        qd = qwrap(q + dq)
        return rcopy(
            msend.at[rows_of(qd)], meta.at[rows_of(q)], m_ssem.at[0], m_rsem.at[0], dev(h, z, c, qd)
        )

    meta_all = rcopy(
        msend.at[pl.ds(0, ROWS - CAP)], msend.at[pl.ds(0, ROWS - CAP)], m_ssem.at[0], m_rsem.at[0], sib
    )

    plane_kinds = [(0, dy) for dy in range(1, NY)] + [(kind, dy) for kind in (1, 2) for dy in range(NY)]
    for kind, dy in plane_kinds:
        disp(kind, dy).start()

    gath[mine, rows_of(q), :] = sent[rows_of(q), :]

    lane8 = lax.broadcasted_iota(jnp.int32, (128, TOK), 0)
    expert = lax.rem(lane8, NE)
    live = lane8 < 3 * NE
    sign = jnp.where(live & (expert == ids_ref[0:1, :]), 1.0, 0.0) - jnp.where(
        live & (expert == ids_ref[1:2, :]), 1.0, 0.0
    )

    @pl.when(c == 0)
    def _():
        w_in_give.start()
        again = lax.broadcasted_iota(jnp.int32, (ROWS, TOK), 0)
        p0 = ids_ref[0:1, :] * CAP + slots_ref[0:1, :]
        p1 = ids_ref[1:2, :] * CAP + slots_ref[1:2, :]
        which = (again == p0).astype(F32) - (again == p1).astype(F32)
        msend[...] = dot_nt(which.astype(BF), sign.astype(BF)).astype(BF)
        for dq in range(1, NE):
            meta_copy(dq).start()
        meta[rows_of(q), :] = msend[rows_of(q), :]

    @pl.when(c == 1)
    def _():
        w_out_give.start()

    pre[...] = jnp.zeros((ROWS, 2 * HID), F32)
    logit[...] = jnp.zeros((ROWS, 128), F32)

    small[2].wait()

    def zblock(hh, d, k):
        return hh * NZ + zwrap(z - k + 2 * d * k)

    def piece(st, d, far):
        rows = second if st == 0 else first
        return rows(d * QUART, QUART) if far else rows()

    def ring(st, d, k, far, back):
        ref = gath.at[zblock(1 - h if st == 2 else h, d, k - back), piece(st, d, far)]
        return rcopy(ref, ref, ag_ssem.at[st, d], ag_rsem.at[st, d, k - 1], znext(d))

    def copy_f(d, k):
        ref = gath.at[zblock(h, d, k), second()]
        return rcopy(ref, ref, f_ssem.at[d], f_rsem.at[d, k], partner)

    def land_f(d, k):
        ref = gath.at[zblock(1 - h, d, k), second()]
        return rcopy(ref, ref, f_ssem.at[d], f_rsem.at[d, k], partner)

    disp_all(0).wait_recv()
    for d in range(2):
        ring(0, d, 1, False, 1).start()
    copy_f(0, 0).start()
    for st in (1, 2):
        disp_all(st).wait_recv()
        for d in range(2):
            ring(st, d, 1, False, 1).start()

    @pl.when(c == 0)
    def _():
        def split(p, carry):
            r = rt_ref[:, lanes(p)]
            top = r.astype(BF).astype(F32)
            mid = (r - top).astype(BF).astype(F32)
            low = r - top - mid
            rt3[:, lanes(p)] = jnp.concatenate([top, mid, low, jnp.zeros((104, BLK), F32)], axis=0).astype(BF)
            return carry

        lax.fori_loop(0, NBLK, split, 0)
        w_in.wait()
        w_out_give.wait_recv()
        meta_all.wait_recv()

    @pl.when(c == 1)
    def _():
        w_out.wait()
        w_in_give.wait_recv()

    def accumulate(p):
        @pl.when(c == 0)
        def _():
            x = gath[p]
            pre[:, 0:HID] += dot_nn(x, wu[0, lanes(p), :])
            pre[:, HID : 2 * HID] += dot_nn(x, wu[1, lanes(p), :])
            logit[...] += dot_nt(x, rt3[:, lanes(p)])

        @pl.when(c == 1)
        def _():
            x = gath[p]
            pre[:, 0:HID] += dot_nt(x, wd[0, :, lanes(p)])
            pre[:, HID : 2 * HID] += dot_nt(x, wd[1, :, lanes(p)])

    def gather_step(k, carry):
        @pl.when((k >= 1) & (k < FAR))
        def _():
            for st in range(3):
                for d in range(2):
                    ring(st, d, k, False, 0).wait_recv()
                    ring(st, d, k, False, 1).wait_send()

                    @pl.when(k < FAR - 1)
                    def _():
                        ring(st, d, k + 1, False, 1).start()

                    @pl.when(k == FAR - 1)
                    def _():
                        ring(st, d, k + 1, True, 1).start()

                    if st == 0:
                        if d == 0:
                            copy_f(0, k - 1).wait_send()
                        else:

                            @pl.when(k > 1)
                            def _():
                                copy_f(1, k - 1).wait_send()

                        copy_f(d, k).start()

        @pl.when(k == FAR)
        def _():
            for st in range(3):
                for d in range(2):
                    ring(st, d, k, True, 0).wait_recv()
                if st == 0:
                    copy_f(1, k - 1).wait_send()
                    copy_f(1, k).start()

        def block_step(j, carry2):
            d = lax.rem(j, 2)
            other = j // 2
            dist = k - other
            ok = (dist >= 0) & (dist <= FAR)
            ok = ok & ((d == 0) | ((dist >= 1) & (dist < FAR)))

            @pl.when(ok)
            def _():
                @pl.when(other == 1)
                def _():
                    dx = jnp.where(dist == FAR, 1, d)
                    land_f(dx, dist).wait_recv()

                accumulate(zblock(lax.rem(h + other, 2), d, dist))

            return carry2

        lax.fori_loop(0, 4, block_step, 0)
        return carry

    lax.fori_loop(0, FAR + 2, gather_step, 0)

    middle = rcopy(ms, mr, mid_sem.at[0], mid_sem.at[1], sib)

    @pl.when(c == 1)
    def _():
        ms[...] = pre[...].astype(BF)

    def gates():
        gap = jnp.sum(logit[...] * meta[...].astype(F32), axis=1, keepdims=True)
        return jax.nn.sigmoid(gap), jax.nn.sigmoid(-gap)

    @pl.when(c == 0)
    def _():
        gate, _ = gates()
        v = pre[...]
        ms[...] = (gate * (v * jax.nn.sigmoid(v))).astype(BF)

    middle.start()
    middle.wait_recv()

    @pl.when(c == 0)
    def _():
        gate, gate_other = gates()
        v = pre[...]
        u = mr[...].astype(F32)
        sg = jax.nn.sigmoid(v)
        pg[...] = (gate * u * (sg * (1.0 + v * (1.0 - sg)))).astype(BF)
        t = jnp.sum(v * sg * u, axis=1, keepdims=True) * gate * gate_other
        ts = t * meta[...].astype(F32)
        top = ts.astype(BF).astype(F32)
        lane = lax.broadcasted_iota(jnp.int32, (ROWS, 128), 1)
        tsb[...] = ts.astype(BF)
        tlb[...] = jnp.where(lane < NE, top, jnp.where(lane < 2 * NE, ts - top, 0.0)).astype(BF)

    def product(p, r):
        @pl.when(c == 0)
        def _():
            acc = dot_nt(pg[r, 0:HID], wu[0, lanes(p), :])
            acc += dot_nt(pg[r, HID : 2 * HID], wu[1, lanes(p), :])
            part[...] = acc + dot_nn(tsb[r, :], rt3[:, lanes(p)])

        @pl.when(c == 1)
        def _():
            acc = dot_nn(mr[r, 0:HID], wd[0, :, lanes(p)])
            part[...] = acc + dot_nn(mr[r, HID : 2 * HID], wd[1, :, lanes(p)])

    def tblock(hh, d, dist):
        return hh * NZ + zwrap(z + dist - 2 * d * dist)

    def sum_piece(d, far):
        return pl.ds(d * QUART, QUART) if far else pl.ds(0, HALF)

    def hop(st, d, t, far):
        rr = sum_piece(d, far)
        return rcopy(
            ring_s.at[st, d, t - 1, rr], ring_r.at[st, d, t - 1, rr], rs_ssem.at[st, d], rs_rsem.at[st, d, t - 1], znext(d)
        )

    def copy_rx(d, dist):
        return rcopy(xs.at[d, dist], xr.at[d, dist], rx_ssem.at[d], rx_rsem.at[d, dist], partner)

    plane = [(dh, dq) for dh in range(2) for dq in range(NE) if dh or dq]

    def plane_dev(dh, dq):
        return lax.rem(h + dh, 2), qwrap(q + dq)

    def copy_g1(i, dh, dq):
        hh, qq = plane_dev(dh, dq)
        return rcopy(gp.at[hh * NE + qq], g1.at[i], g1_ssem.at[0], g1_rsem.at[0], dev(hh, z, c, qq))

    def copy_g2(dz):
        return rcopy(g2s, g2.at[dz], g2_ssem.at[0], g2_rsem.at[0], dev(h, zwrap(z + dz), c, q))

    me_p = h * NE + q

    def copy_g3(i, dh, dq):
        hh, qq = plane_dev(dh, dq)
        return rcopy(g3s, g3.at[:, lanes(me_p)], g3_ssem.at[0], g3_rsem.at[0], dev(hh, z, c, qq))

    all_g1 = rcopy(g1, g1, g1_ssem.at[0], g1_rsem.at[0], sib)
    near_g2 = g2.at[pl.ds(1, NZ - 1)]
    all_g2 = rcopy(near_g2, near_g2, g2_ssem.at[0], g2_rsem.at[0], sib)
    all_g3 = rcopy(g1, g1, g3_ssem.at[0], g3_rsem.at[0], sib)

    g4 = rcopy(g3, gr_ref, g4_sem.at[0], g4_sem.at[1], sib)
    g4_own = pltpu.make_async_copy(g3, gr_ref, g4_sem.at[2])

    def router_stage(step):
        @pl.when((c == 0) & ((step == 1) | (step == 2)))
        def _():
            tl = tlb[...]

            def one(p, carry):
                full = dot_tn(tl, gath[p])
                gp[p] = full[0:NE] + full[NE : 2 * NE]
                return carry

            lax.fori_loop((step - 1) * (NBLK // 2), step * (NBLK // 2), one, 0)

        @pl.when((c == 0) & (step == 2))
        def _():
            for i, (dh, dq) in enumerate(plane):
                copy_g1(i, dh, dq).start()

        @pl.when((c == 0) & (step == FAR - 1))
        def _():
            total = gp[me_p]
            all_g1.wait_recv()
            for i in range(len(plane)):
                total = total + g1[i]
            g2s[...] = total
            for dz in range(1, NZ):
                copy_g2(dz).start()

        @pl.when((c == 0) & (step == FAR))
        def _():
            total = g2s[...]
            all_g2.wait_recv()
            for dz in range(1, NZ):
                total = total + g2[dz]
            g3s[...] = total
            g3[:, lanes(me_p)] = total
            for i, (dh, dq) in enumerate(plane):
                copy_g3(i, dh, dq).start()

        @pl.when((c == 0) & (step == FAR + 1))
        def _():
            all_g3.wait_recv()
            g4.start()
            g4_own.start()

    gu_own = pltpu.make_async_copy(gu0, gu_ref, gsem.at[0])
    gd_own = pltpu.make_async_copy(gd0, gd_ref, gsem.at[0])
    gu_give = rcopy(gu, gu_ref, gsem.at[1], gsem.at[2], sib)
    gd_give = rcopy(gd, gd_ref, gsem.at[1], gsem.at[2], sib)

    def weight_grads(step):
        def one(i, carry):
            p = (step - 1) * 4 + i

            @pl.when(c == 0)
            def _():
                full = dot_tn(gath[p], pg[...]).astype(BF)
                gu0[lanes(p), :] = full[:, 0:HID]
                gu[lanes(p), :] = full[:, HID : 2 * HID]

            @pl.when(c == 1)
            def _():
                full = dot_tn(mr[...], gath[p]).astype(BF)
                gd[:, lanes(p)] = full[0:HID]
                gd0[:, lanes(p)] = full[HID : 2 * HID]

            return carry

        @pl.when((step >= 1) & (step <= FAR))
        def _():
            lax.fori_loop(0, 4, one, 0)

        @pl.when((step == FAR) & (c == 0))
        def _():
            gu_own.start()
            gu_give.start()

        @pl.when((step == FAR) & (c == 1))
        def _():
            gd_own.start()
            gd_give.start()

    def ret_copy(kind, dy):
        qd = group(kind == 0, dy)
        sems = r_ssem.at[kind], r_rsem.at[kind]
        if kind == 2:
            return rcopy(fs1.at[rows_of(lax.rem(qd, NY))], ret1.at[rows_of(y)], *sems, dev(1 - h, z, c, qd))
        return rcopy(fs0.at[rows_of(qd)], ret0.at[rows_of(q)], *sems, dev(h, z, c, qd))

    def ret_all(kind):
        ref = rows_in(fs0, kind)
        return rcopy(ref, ref, r_ssem.at[kind], r_rsem.at[kind], sib)

    last = FAR + 1

    def scatter_step(step, carry):
        nxt = FAR - step

        def share(d, carry2):
            @pl.when(((step == 0) & (d == 1)) | ((step >= 1) & (step < FAR)) | ((step == FAR) & (d == 0)))
            def _():
                product(tblock(1 - h, d, nxt), second())
                xs[d, nxt] = part[...].astype(BF)

                @pl.when(step >= 1 + (1 - d))
                def _():
                    copy_rx(d, nxt + 1).wait_send()

                copy_rx(d, nxt).start()

            return carry2

        def stream(st, step):
            hh = 1 - h if st == 2 else h
            dist = last - step

            def one(d, carry2):
                @pl.when((((step == 1) | (step == last)) & (d == 0)) | ((step > 1) & (step < last)))
                def _():
                    product(tblock(hh, d, dist), second() if st == 0 else first())
                    total = part[...]
                    if st == 0:
                        far_d = jnp.where(step == 1, 1, d)
                        copy_rx(far_d, dist).wait_recv()
                        total = total + xr[far_d, dist].astype(F32)

                    @pl.when(step == 1)
                    def _():
                        for dd in range(2):
                            rr = slice(dd * QUART, (dd + 1) * QUART)
                            ring_s[st, dd, 0, rr] = total[rr].astype(BF)
                            hop(st, dd, 1, True).start()

                    @pl.when(step == 2)
                    def _():
                        hop(st, d, 1, True).wait_recv()
                        hop(st, d, 1, True).wait_send()
                        ring_s[st, d, 1] = total.astype(BF)
                        rr = pl.ds(d * QUART, QUART)
                        part[...] = total
                        got = part[rr, :] + ring_r[st, d, 0, rr, :].astype(F32)
                        ring_s[st, d, 1, rr, :] = got.astype(BF)
                        hop(st, d, 2, False).start()

                    @pl.when((step > 2) & (step < last))
                    def _():
                        hop(st, d, step - 1, False).wait_recv()
                        hop(st, d, step - 1, False).wait_send()
                        ring_s[st, d, step - 1] = (total + ring_r[st, d, step - 2].astype(F32)).astype(BF)
                        hop(st, d, step, False).start()

                    @pl.when(step == last)
                    def _():
                        hop(st, 0, FAR, False).wait_recv()
                        hop(st, 1, FAR, False).wait_recv()
                        got = total + ring_r[st, 0, FAR - 1].astype(F32) + ring_r[st, 1, FAR - 1].astype(F32)
                        if st == 2:
                            fs1[...] = got.astype(BF)
                        else:
                            fs0[second() if st == 0 else first(), :] = got.astype(BF)
                        for dy in range(NY):
                            if st == 0 and dy == 0:
                                ret0[rows_of(q), :] = fs0[rows_of(q), :]
                            else:
                                ret_copy(st, dy).start()

                return carry2

            lax.fori_loop(0, 2, one, 0)

        stream(1, step)

        @pl.when(step == FAR)
        def _():
            stream(0, step - 1)

        stream(2, step)
        lax.fori_loop(0, 2, share, 0)

        @pl.when(step == 1)
        def _():
            router_stage(step)
            weight_grads(step)

        stream(0, jnp.where(step < FAR, step - 1, step))

        @pl.when(step > 1)
        def _():
            router_stage(step)
            weight_grads(step)

        return carry

    lax.fori_loop(0, last + 1, scatter_step, 0)

    for kind in (1, 2, 0):
        ret_all(kind).wait_recv()
    got = dot_tn(pick[...], ret0[...]) + dot_tn(pick[first(), :], ret1[...])
    rounded = got.astype(BF)
    trade.wait_send()
    give[...] = dot_nt(rounded, place_other).astype(BF)
    give_tokens = rcopy(give, og_ref, o_sem.at[0], o_sem.at[1], sib)
    give_mixed = rcopy(give, om_ref, o_sem.at[0], o_sem.at[1], sib)
    put_tokens = pltpu.make_async_copy(keep, og_ref, o_sem.at[2])
    put_mixed = pltpu.make_async_copy(keep, om_ref, o_sem.at[2])

    @pl.when(c == 0)
    def _():
        give_tokens.start()

    @pl.when(c == 1)
    def _():
        give_mixed.start()

    keep[...] = dot_nt(rounded, place_mine).astype(BF)

    @pl.when(c == 0)
    def _():
        put_tokens.start()

    @pl.when(c == 1)
    def _():
        put_mixed.start()

    for kind in range(3):
        disp_all(kind).wait_send()
        ret_all(kind).wait_send()

    for d in range(2):
        for st in range(3):
            ring(st, d, FAR, True, 1).wait_send()
            hop(st, d, FAR, False).wait_send()
    copy_f(0, FAR - 1).wait_send()
    copy_f(1, FAR).wait_send()
    copy_rx(0, 0).wait_send()
    copy_rx(1, 1).wait_send()
    middle.wait_send()

    @pl.when(c == 0)
    def _():
        w_in_give.wait_send()
        meta_all.wait_send()
        all_g1.wait_send()
        all_g2.wait_send()
        all_g3.wait_send()
        g4.wait_send()
        g4_own.wait()
        gu_own.wait()
        gu_give.wait_send()
        gd_give.wait_recv()

    @pl.when(c == 1)
    def _():
        w_out_give.wait_send()
        g4.wait_recv()
        gd_own.wait()
        gd_give.wait_send()
        gu_give.wait_recv()

    @pl.when(c == 0)
    def _():
        put_tokens.wait()
        give_tokens.wait_send()
        give_mixed.wait_recv()

    @pl.when(c == 1)
    def _():
        put_mixed.wait()
        give_mixed.wait_send()
        give_tokens.wait_recv()


def vm(*shape, dtype=BF):
    return pltpu.VMEM(shape, dtype)


def dma(*shape):
    return pltpu.SemaphoreType.DMA(shape)


def store(om, og, gu, gd, gr, om_out, og_out, gu_out, gd_out, gr_out, sem):
    copies = [
        pltpu.make_async_copy(src, dst, sem.at[i])
        for i, (src, dst) in enumerate(((gu, gu_out), (gd, gd_out), (om, om_out), (og, og_out), (gr, gr_out)))
    ]
    for copy in copies:
        copy.start()
    for copy in copies:
        copy.wait()


def shards(tokens, expert_ids, slot_ids, router, up_weight, down_weight, cotangent):
    aspec = pl.BlockSpec(memory_space=pl.ANY)
    hspec = pl.BlockSpec(memory_space=pltpu.HBM)
    shapes = (
        jax.ShapeDtypeStruct((TOK, FEAT), BF),
        jax.ShapeDtypeStruct((TOK, FEAT), BF),
        jax.ShapeDtypeStruct((WIDTH, HID), BF),
        jax.ShapeDtypeStruct((HID, WIDTH), BF),
        jax.ShapeDtypeStruct((NE, WIDTH), F32),
    )
    results = pl.pallas_call(
        kernel,
        out_shape=(
            *shapes,
        ),
        in_specs=[hspec] * 7,
        out_specs=(aspec,) * 5,
        scratch_shapes=[
            vm(NBLK, ROWS, BLK), vm(2, WIDTH, HID), vm(2, HID, WIDTH), vm(WIDTH, HID), vm(HID, WIDTH), vm(WIDTH, HID), vm(HID, WIDTH),
            vm(128, WIDTH), vm(ROWS, TOK), vm(TOK, FEAT), vm(TOK, FEAT),
            vm(2, TOK, dtype=jnp.int32), vm(2, TOK, dtype=jnp.int32), vm(NE, WIDTH, dtype=F32),
            vm(TOK, FEAT), vm(ROWS, BLK), vm(ROWS, 128), vm(ROWS, 128),
            vm(ROWS, 2 * HID, dtype=F32), vm(ROWS, 128, dtype=F32), vm(ROWS, 2 * HID), vm(ROWS, 2 * HID),
            vm(ROWS, 2 * HID), vm(ROWS, 128), vm(ROWS, 128), vm(HALF, BLK, dtype=F32),
            vm(3, 2, FAR, HALF, BLK), vm(3, 2, FAR, HALF, BLK), vm(2, 5, HALF, BLK), vm(2, 5, HALF, BLK),
            vm(ROWS, BLK), vm(HALF, BLK), vm(ROWS, BLK), vm(HALF, BLK),
            vm(NBLK, NE, BLK, dtype=F32), vm(15, NE, BLK, dtype=F32), vm(NE, BLK, dtype=F32),
            vm(NZ, NE, BLK, dtype=F32), vm(NE, BLK, dtype=F32), vm(NE, WIDTH, dtype=F32),
            dma(5), dma(3), dma(2), dma(3), dma(3), dma(1), dma(1),
            dma(3, 2), dma(3, 2, FAR), dma(2), dma(2, 5), dma(2), dma(3, 2), dma(3, 2, FAR), dma(2), dma(2, 5),
            dma(3), dma(3), dma(3), dma(3),
            dma(1), dma(1), dma(1), dma(1), dma(1), dma(1), dma(3),
        ],
        compiler_params=pltpu.CompilerParams(
            collective_id=0, has_side_effects=True, vmem_limit_bytes=47 << 20
        ),
    )(
        *(
            pltpu.with_memory_space_constraint(v, pltpu.HBM)
            for v in (tokens, cotangent, expert_ids.T, slot_ids.T, router.T, up_weight[0], down_weight[0])
        )
    )
    mixed, grad_tokens, gu, gd, gr = pl.pallas_call(
        store,
        out_shape=shapes,
        in_specs=[aspec] * 5,
        out_specs=(hspec,) * 5,
        scratch_shapes=[dma(5)],
        compiler_params=pltpu.CompilerParams(vmem_limit_bytes=1 << 20),
    )(*results)
    return (mixed, grad_tokens, gu[None], gd[None], gr.T)


def solution(mesh):
    in_specs = (
        P("expert", "section"),
        P("expert", None),
        P("expert", None),
        P(),
        P("expert", None, "section"),
        P("expert", "section", None),
        P("expert", "section"),
    )
    out_specs = (
        P("expert", "section"),
        P("expert", "section"),
        P("expert", None, "section"),
        P("expert", "section", None),
        P(),
    )
    return jax.shard_map(shards, mesh=mesh, in_specs=in_specs, out_specs=out_specs, check_vma=False)
```

time: 116 us -> 113 us (0.974)
  Pallas kernels: 115 us -> 112 us
    pallas_call x1, Pallas kernels: 112 us -> 109 us  [shards(): pl.pallas_call(kernel, out_shape=(*shapes,), in_specs=[hspec] * 7, out_sp...]
where the time goes in v3:
time: 113 us; the launch traced here: 112 us
  Pallas kernels  112 us (99%)
    pallas_call x1, Pallas kernels, shards(): pl.pallas_call(kernel, out_shape=(*shapes,), in_specs=[hspec] * 7, out_sp...  109 us
    pallas_call x1, Pallas kernels, shards(): pl.pallas_call(store, out_shape=shapes, in_specs=[aspec] * 5, out_specs=(...  2.85 us

profile of v3, /device:TPU:1, one launch (start us, length us, event | category | flops | bytes accessed | tf_op | source)
XLA Modules:
  0.0 112.5 jit_solution(1530958429163079765)
XLA Ops:
  0.6 109.0 %shard_map.110 = (bf16[192,192]{1,0:T(8,128)(2,1)S(1)}, bf16[192,192]{1,0:T(8,128)(2,1)S(1)}, bf16[6144,256]{1,0:T(8,128)(2,1)S(1)}, bf16[256,6144]{1,0:T(8,128)(2,1)S(1)}, f32[8,6144]{1,0:T(8,128)S(1)}) custom-call(bf16[192,192]{1,0:T(8,128)(2,1)} %tok_ref.1, bf16[192,192]{1,0:T(8,128)(2,1)} %cot_ref.1, s32[2,192]{1,0:T(2,128)} %bitcast.11, ...), custom_call_target="tpu_custom_call" | custom-call | tf_op jit(solution)/shard_map/pallas_call | solution.py:736
  109.6 2.9 %shard_map.111 = (bf16[192,192]{1,0:T(8,128)(2,1)}, bf16[192,192]{1,0:T(8,128)(2,1)}, bf16[6144,256]{1,0:T(8,128)(2,1)}, bf16[256,6144]{1,0:T(8,128)(2,1)}, f32[8,6144]{1,0:T(8,128)}) custom-call(bf16[192,192]{1,0:T(8,128)(2,1)S(1)} %get-tuple-element.15.om, bf16[192,192]{1,0:T(8,128)(2,1)S(1)} %get-tuple-element.16.og, ...), custom_call_target="tpu_custom_call" | custom-call | tf_op jit(solution)/shard_map/pallas_call | solution.py:768

commit v4 on v3

--- a/solution.py
+++ b/solution.py
@@ -192,7 +192,7 @@
         msend.at[pl.ds(0, ROWS - CAP)], msend.at[pl.ds(0, ROWS - CAP)], m_ssem.at[0], m_rsem.at[0], sib
     )
 
-    plane_kinds = [(0, dy) for dy in range(1, NY)] + [(kind, dy) for kind in (1, 2) for dy in range(NY)]
+    plane_kinds = [(0, 2), (0, 1), (0, 3)] + [(kind, dy) for kind in (1, 2) for dy in (2, 1, 3, 0)]
     for kind, dy in plane_kinds:
         disp(kind, dy).start()
 
@@ -405,7 +405,7 @@
         )
 
     def copy_rx(d, dist):
-        return rcopy(xs.at[d, dist], xr.at[d, dist], rx_ssem.at[d], rx_rsem.at[d, dist], partner)
+        return rcopy(xs.at[d, dist], xr.at[d, dist], rx_ssem.at[d, dist], rx_rsem.at[d, dist], partner)
 
     plane = [(dh, dq) for dh in range(2) for dq in range(NE) if dh or dq]
 
@@ -433,49 +433,41 @@
     g4 = rcopy(g3, gr_ref, g4_sem.at[0], g4_sem.at[1], sib)
     g4_own = pltpu.make_async_copy(g3, gr_ref, g4_sem.at[2])
 
-    def router_stage(step):
-        @pl.when((c == 0) & ((step == 1) | (step == 2)))
-        def _():
-            tl = tlb[...]
-
-            def one(p, carry):
-                full = dot_tn(tl, gath[p])
-                gp[p] = full[0:NE] + full[NE : 2 * NE]
-                return carry
-
-            lax.fori_loop((step - 1) * (NBLK // 2), step * (NBLK // 2), one, 0)
-
-        @pl.when((c == 0) & (step == 2))
-        def _():
-            for i, (dh, dq) in enumerate(plane):
-                copy_g1(i, dh, dq).start()
-
-        @pl.when((c == 0) & (step == FAR - 1))
-        def _():
-            total = gp[me_p]
-            all_g1.wait_recv()
-            for i in range(len(plane)):
-                total = total + g1[i]
-            g2s[...] = total
-            for dz in range(1, NZ):
-                copy_g2(dz).start()
-
-        @pl.when((c == 0) & (step == FAR))
-        def _():
-            total = g2s[...]
-            all_g2.wait_recv()
-            for dz in range(1, NZ):
-                total = total + g2[dz]
-            g3s[...] = total
-            g3[:, lanes(me_p)] = total
-            for i, (dh, dq) in enumerate(plane):
-                copy_g3(i, dh, dq).start()
-
-        @pl.when((c == 0) & (step == FAR + 1))
-        def _():
-            all_g3.wait_recv()
-            g4.start()
-            g4_own.start()
+    def router_parts():
+        tl = tlb[...]
+
+        def one(p, carry):
+            full = dot_tn(tl, gath[p])
+            gp[p] = full[0:NE] + full[NE : 2 * NE]
+            return carry
+
+        lax.fori_loop(0, NBLK, one, 0)
+        for i, (dh, dq) in enumerate(plane):
+            copy_g1(i, dh, dq).start()
+
+    def router_plane():
+        all_g1.wait_recv()
+        total = gp[me_p]
+        for i in range(len(plane)):
+            total = total + g1[i]
+        g2s[...] = total
+        for dz in range(1, NZ):
+            copy_g2(dz).start()
+
+    def router_column():
+        all_g2.wait_recv()
+        total = g2s[...]
+        for dz in range(1, NZ):
+            total = total + g2[dz]
+        g3s[...] = total
+        g3[:, lanes(me_p)] = total
+        for i, (dh, dq) in enumerate(plane):
+            copy_g3(i, dh, dq).start()
+
+    def router_out():
+        all_g3.wait_recv()
+        g4.start()
+        g4_own.start()
 
     gu_own = pltpu.make_async_copy(gu0, gu_ref, gsem.at[0])
     gd_own = pltpu.make_async_copy(gd0, gd_ref, gsem.at[0])
@@ -483,9 +475,7 @@
     gd_give = rcopy(gd, gd_ref, gsem.at[1], gsem.at[2], sib)
 
     def weight_grads(step):
-        def one(i, carry):
-            p = (step - 1) * 4 + i
-
+        def one(p, carry):
             @pl.when(c == 0)
             def _():
                 full = dot_tn(gath[p], pg[...]).astype(BF)
@@ -500,9 +490,12 @@
 
             return carry
 
-        @pl.when((step >= 1) & (step <= FAR))
-        def _():
-            lax.fori_loop(0, 4, one, 0)
+        begin = jnp.where(step == 1, 0, jnp.where(step == FAR - 1, 4, 10))
+        end = jnp.where(step == 1, 4, jnp.where(step == FAR - 1, 10, NBLK))
+
+        @pl.when((step == 1) | (step == FAR - 1) | (step == FAR))
+        def _():
+            lax.fori_loop(begin, end, one, 0)
 
         @pl.when((step == FAR) & (c == 0))
         def _():
@@ -535,11 +528,6 @@
             def _():
                 product(tblock(1 - h, d, nxt), second())
                 xs[d, nxt] = part[...].astype(BF)
-
-                @pl.when(step >= 1 + (1 - d))
-                def _():
-                    copy_rx(d, nxt + 1).wait_send()
-
                 copy_rx(d, nxt).start()
 
             return carry2
@@ -606,30 +594,34 @@
 
         @pl.when(step == FAR)
         def _():
+            @pl.when(c == 0)
+            def _():
+                router_plane()
+
             stream(0, step - 1)
 
         stream(2, step)
         lax.fori_loop(0, 2, share, 0)
-
-        @pl.when(step == 1)
-        def _():
-            router_stage(step)
-            weight_grads(step)
-
         stream(0, jnp.where(step < FAR, step - 1, step))
 
-        @pl.when(step > 1)
-        def _():
-            router_stage(step)
-            weight_grads(step)
-
+        @pl.when((step == 2) & (c == 0))
+        def _():
+            router_parts()
+
+        @pl.when((step == FAR) & (c == 0))
+        def _():
+            router_column()
+
+        weight_grads(step)
         return carry
 
     lax.fori_loop(0, last + 1, scatter_step, 0)
 
-    for kind in (1, 2, 0):
+    for kind in (1, 2):
         ret_all(kind).wait_recv()
-    got = dot_tn(pick[...], ret0[...]) + dot_tn(pick[first(), :], ret1[...])
+    got = dot_tn(pick[first(), :], ret0[first(), :]) + dot_tn(pick[first(), :], ret1[...])
+    ret_all(0).wait_recv()
+    got = got + dot_tn(pick[second(), :], ret0[second(), :])
     rounded = got.astype(BF)
     trade.wait_send()
     give[...] = dot_nt(rounded, place_other).astype(BF)
@@ -651,6 +643,7 @@
     @pl.when(c == 0)
     def _():
         put_tokens.start()
+        router_out()
 
     @pl.when(c == 1)
     def _():
@@ -666,8 +659,9 @@
             hop(st, d, FAR, False).wait_send()
     copy_f(0, FAR - 1).wait_send()
     copy_f(1, FAR).wait_send()
-    copy_rx(0, 0).wait_send()
-    copy_rx(1, 1).wait_send()
+    for k in range(FAR):
+        copy_rx(0, k).wait_send()
+        copy_rx(1, k + 1).wait_send()
     middle.wait_send()
 
     @pl.when(c == 0)
@@ -752,7 +746,7 @@
             vm(NBLK, NE, BLK, dtype=F32), vm(15, NE, BLK, dtype=F32), vm(NE, BLK, dtype=F32),
             vm(NZ, NE, BLK, dtype=F32), vm(NE, BLK, dtype=F32), vm(NE, WIDTH, dtype=F32),
             dma(5), dma(3), dma(2), dma(3), dma(3), dma(1), dma(1),
-            dma(3, 2), dma(3, 2, FAR), dma(2), dma(2, 5), dma(2), dma(3, 2), dma(3, 2, FAR), dma(2), dma(2, 5),
+            dma(3, 2), dma(3, 2, FAR), dma(2), dma(2, 5), dma(2), dma(3, 2), dma(3, 2, FAR), dma(2, 5), dma(2, 5),
             dma(3), dma(3), dma(3), dma(3),
             dma(1), dma(1), dma(1), dma(1), dma(1), dma(1), dma(3),
         ],

time: 113 us -> 110 us (0.973)
  Pallas kernels: 112 us -> 110 us
    pallas_call x1, Pallas kernels: 109 us -> 107 us  [shards(): pl.pallas_call(kernel, out_shape=(*shapes,), in_specs=[hspec] * 7, out_sp...]
where the time goes in v4:
time: 110 us
  Pallas kernels  110 us (100%)
    pallas_call x1, Pallas kernels, shards(): pl.pallas_call(kernel, out_shape=(*shapes,), in_specs=[hspec] * 7, out_sp...  107 us
    pallas_call x1, Pallas kernels, shards(): pl.pallas_call(store, out_shape=shapes, in_specs=[aspec] * 5, out_specs=(...  2.85 us

profile of v4, /device:TPU:1, one launch (start us, length us, event | category | flops | bytes accessed | tf_op | source)
XLA Modules:
  0.0 110.3 jit_solution(12971746631282732260)
XLA Ops:
  0.6 106.8 %shard_map.110 = (bf16[192,192]{1,0:T(8,128)(2,1)S(1)}, bf16[192,192]{1,0:T(8,128)(2,1)S(1)}, bf16[6144,256]{1,0:T(8,128)(2,1)S(1)}, bf16[256,6144]{1,0:T(8,128)(2,1)S(1)}, f32[8,6144]{1,0:T(8,128)S(1)}) custom-call(bf16[192,192]{1,0:T(8,128)(2,1)} %tok_ref.1, bf16[192,192]{1,0:T(8,128)(2,1)} %cot_ref.1, s32[2,192]{1,0:T(2,128)} %bitcast.11, ...), custom_call_target="tpu_custom_call" | custom-call | tf_op jit(solution)/shard_map/pallas_call | solution.py:730
  107.4 2.9 %shard_map.111 = (bf16[192,192]{1,0:T(8,128)(2,1)}, bf16[192,192]{1,0:T(8,128)(2,1)}, bf16[6144,256]{1,0:T(8,128)(2,1)}, bf16[256,6144]{1,0:T(8,128)(2,1)}, f32[8,6144]{1,0:T(8,128)}) custom-call(bf16[192,192]{1,0:T(8,128)(2,1)S(1)} %get-tuple-element.15.om, bf16[192,192]{1,0:T(8,128)(2,1)S(1)} %get-tuple-element.16.og, ...), custom_call_target="tpu_custom_call" | custom-call | tf_op jit(solution)/shard_map/pallas_call | solution.py:762

commit v5 on v4

--- a/solution.py
+++ b/solution.py
@@ -114,9 +114,7 @@
     for copy in small:
         copy.start()
     tok_keep = pltpu.make_async_copy(tok_ref, keep, in_sem.at[3])
-    cot_give = pltpu.make_async_copy(cot_ref, give, in_sem.at[4])
     cot_keep = pltpu.make_async_copy(cot_ref, keep, in_sem.at[3])
-    tok_give = pltpu.make_async_copy(tok_ref, give, in_sem.at[4])
     w_in = pltpu.make_async_copy(up_ref, wu.at[0], w_sem.at[0])
     w_in_give = rcopy(dn_ref, wd.at[0], w_sem.at[1], w_sem.at[2], sib)
     w_out = pltpu.make_async_copy(dn_ref, wd.at[1], w_sem.at[0])
@@ -124,29 +122,28 @@
 
     @pl.when(c == 0)
     def _():
-        cot_give.start()
         tok_keep.start()
         w_in.start()
 
     @pl.when(c == 1)
     def _():
-        tok_give.start()
         cot_keep.start()
         w_out.start()
 
-    @pl.when(c == 0)
-    def _():
-        cot_give.wait()
+    pl.semaphore_wait(barrier, len(peers))
+    trade = rcopy(cot_ref, xch, x_sem.at[0], x_sem.at[1], sib)
+    trade_back = rcopy(tok_ref, xch, x_sem.at[0], x_sem.at[1], sib)
+
+    @pl.when(c == 0)
+    def _():
+        trade.start()
         tok_keep.wait()
 
     @pl.when(c == 1)
     def _():
-        tok_give.wait()
+        trade_back.start()
         cot_keep.wait()
 
-    pl.semaphore_wait(barrier, len(peers))
-    trade = rcopy(give, xch, x_sem.at[0], x_sem.at[1], sib)
-    trade.start()
     row = lax.broadcasted_iota(jnp.int32, (FEAT, BLK), 0)
     col = lax.broadcasted_iota(jnp.int32, (FEAT, BLK), 1)
     place_mine = (col == row + FEAT * c).astype(F32).astype(BF)
@@ -745,7 +742,7 @@
             vm(ROWS, BLK), vm(HALF, BLK), vm(ROWS, BLK), vm(HALF, BLK),
             vm(NBLK, NE, BLK, dtype=F32), vm(15, NE, BLK, dtype=F32), vm(NE, BLK, dtype=F32),
             vm(NZ, NE, BLK, dtype=F32), vm(NE, BLK, dtype=F32), vm(NE, WIDTH, dtype=F32),
-            dma(5), dma(3), dma(2), dma(3), dma(3), dma(1), dma(1),
+            dma(4), dma(3), dma(2), dma(3), dma(3), dma(1), dma(1),
             dma(3, 2), dma(3, 2, FAR), dma(2), dma(2, 5), dma(2), dma(3, 2), dma(3, 2, FAR), dma(2, 5), dma(2, 5),
             dma(3), dma(3), dma(3), dma(3),
             dma(1), dma(1), dma(1), dma(1), dma(1), dma(1), dma(3),

time: 110 us -> 111 us (level)
  no operation moved by 1% of the time
where the time goes in v5:
time: 111 us; the launch traced here: 110 us
  Pallas kernels  110 us (99%)
    pallas_call x1, Pallas kernels, shards(): pl.pallas_call(kernel, out_shape=(*shapes,), in_specs=[hspec] * 7, out_sp...  107 us
    pallas_call x1, Pallas kernels, shards(): pl.pallas_call(store, out_shape=shapes, in_specs=[aspec] * 5, out_specs=(...  2.85 us

profile of v5, /device:TPU:1, one launch (start us, length us, event | category | flops | bytes accessed | tf_op | source)
XLA Modules:
  0.0 110.5 jit_solution(12231906031431292642)
XLA Ops:
  0.6 107.0 %shard_map.110 = (bf16[192,192]{1,0:T(8,128)(2,1)S(1)}, bf16[192,192]{1,0:T(8,128)(2,1)S(1)}, bf16[6144,256]{1,0:T(8,128)(2,1)S(1)}, bf16[256,6144]{1,0:T(8,128)(2,1)S(1)}, f32[8,6144]{1,0:T(8,128)S(1)}) custom-call(bf16[192,192]{1,0:T(8,128)(2,1)} %tok_ref.1, bf16[192,192]{1,0:T(8,128)(2,1)} %cot_ref.1, s32[2,192]{1,0:T(2,128)} %bitcast.11, ...), custom_call_target="tpu_custom_call" | custom-call | tf_op jit(solution)/shard_map/pallas_call | solution.py:727
  107.6 2.9 %shard_map.111 = (bf16[192,192]{1,0:T(8,128)(2,1)}, bf16[192,192]{1,0:T(8,128)(2,1)}, bf16[6144,256]{1,0:T(8,128)(2,1)}, bf16[256,6144]{1,0:T(8,128)(2,1)}, f32[8,6144]{1,0:T(8,128)}) custom-call(bf16[192,192]{1,0:T(8,128)(2,1)S(1)} %get-tuple-element.15.om, bf16[192,192]{1,0:T(8,128)(2,1)S(1)} %get-tuple-element.16.og, ...), custom_call_target="tpu_custom_call" | custom-call | tf_op jit(solution)/shard_map/pallas_call | solution.py:759
